TPU v7x, 256 devices: a whole 4x4x8 slice. The times are simulated.
256 devices in a mesh: section: 4 (over y), band: 32 (over x, z), members: 2 (over core).
Axes of the slice: x: 4, y: 4, z: 8, core: 2. Of those that a mesh axis runs over, the one named last changes fastest.
Arguments:
- fields: bfloat16 [8, 128, 576, 128], P(('members', 'section'), 'band'), parts along dimension 0, may hold values from -6 to 6
- lat_taps: bfloat16 [2, 9, 128], replicated, may hold values from -1.5 to 1.5
- lon_taps: bfloat16 [2, 9, 128], replicated, may hold values from -1.5 to 1.5
- gains: float32 [2, 128], replicated, may hold values from 0.1 to 1.9
- w_in: bfloat16 [2, 128, 256], replicated, may hold values from -0.5 to 0.5
- w_out: bfloat16 [2, 256, 128], replicated, may hold values from -0.375 to 0.375
Outputs:
- final_states: bfloat16 [8, 128, 576, 128], P(('members', 'section'), 'band'), parts along dimension 0
There are 2 independent parts, one for each index of `members`. A program takes and returns all parts, laid end to end along the dimension named above; an argument that names none is the same for every part. Nothing has to cross between parts.
All inputs are finite; a program needn't handle non-finite values.
Results may differ from a plain program's by a relative error of at most 0.0063.
Values may be sent and summed in bfloat16 or wider, within the bound.
A program may use at most 64 MiB of HBM per device.

v0:
```python
import jax
import jax.numpy as jnp
from jax import lax
from jax.sharding import PartitionSpec as P

DLON = 3
LAYERS = 2


def column_mix(padded, lat_w, rows):
    lat_tap = lat_w.astype(jnp.float32)
    total = jnp.zeros(padded.shape[:1] + (rows,) + padded.shape[2:], jnp.float32)
    for k in range(9):
        total = total + padded[:, k : k + rows].astype(jnp.float32) * lat_tap[k]
    return total.astype(jnp.bfloat16)


def layer_rest(state, latmix, lon_w, gain, proj_in, proj_out):
    lon_tap = lon_w.astype(jnp.float32)
    lonmix = jnp.zeros(latmix.shape, jnp.float32)
    for k in range(9):
        lonmix = lonmix + jnp.roll(latmix, -DLON * (k - 4), axis=2).astype(jnp.float32) * lon_tap[k]
    mean = jnp.mean(lonmix, axis=-1, keepdims=True)
    centred = lonmix - mean
    var = jnp.mean(centred * centred, axis=-1, keepdims=True)
    normed = (centred / jnp.sqrt(var + 1e-06) * gain).astype(jnp.bfloat16)
    flat = normed.reshape(-1, normed.shape[-1])
    hidden = jax.nn.gelu(
        jnp.dot(flat, proj_in, preferred_element_type=jnp.float32), approximate=False
    ).astype(jnp.bfloat16)
    delta = jnp.dot(hidden, proj_out, preferred_element_type=jnp.float32).reshape(latmix.shape)
    return (state.astype(jnp.float32) + delta).astype(jnp.bfloat16)


def shards(fields, lat_taps, lon_taps, gains, w_in, w_out):
    state = fields
    for layer in range(LAYERS):
        lat_w = lat_taps[layer]
        columns = lax.all_to_all(state, "band", split_axis=2, concat_axis=1, tiled=True)
        padded = jnp.pad(columns, ((0, 0), (4, 4), (0, 0), (0, 0)))
        mixed = column_mix(padded, lat_w, columns.shape[1])
        latmix = lax.all_to_all(mixed, "band", split_axis=1, concat_axis=2, tiled=True)
        state = layer_rest(state, latmix, lon_taps[layer], gains[layer], w_in[layer], w_out[layer])
    return state


def solution(mesh):
    return jax.shard_map(
        shards,
        mesh=mesh,
        in_specs=(P(("members", "section"), "band", None, None), P(), P(), P(), P(), P()),
        out_specs=P(("members", "section"), "band", None, None),
        check_vma=False,
    )
```

profile of v0, /device:TPU:6, one launch (start us, length us, event | category | flops | bytes accessed | tf_op | source)
XLA Modules:
  0.0 179.6 jit_solution(4117968349406515064)
XLA Ops:
  0.0 2.3 %copy.91 = bf16[1,4,576,128]{3,1,0,2:T(4,128)(2,1)} copy(bf16[1,4,576,128]{3,2,1,0:T(8,128)(2,1)} %param.6) | data formatting | bytes 1179648 | tf_op args[0]
  2.4 11.6 %all-to-all-start = ((bf16[1,4,576,128]{3,1,0,2:T(4,128)(2,1)}), bf16[1,4,576,128]{3,1,0,2:T(4,128)(2,1)S(1)}, u32[]{:S(2)}, u32[]{:S(2)}) async-start(bf16[1,4,576,128]{3,1,0,2:T(4,128)(2,1)} %copy.91), calls=%async_computation | async-start | bytes 1179648 | tf_op jit(solution)/shard_map/all_to_all | solution.py:39
  14.0 16.3 %all-to-all-done = bf16[1,4,576,128]{3,1,0,2:T(4,128)(2,1)S(1)} async-done(((bf16[1,4,576,128]{3,1,0,2:T(4,128)(2,1)}), bf16[1,4,576,128]{3,1,0,2:T(4,128)(2,1)S(1)}, u32[]{:S(2)}, u32[]{:S(2)}) %all-to-all-start) | async-done | bytes 589856 | tf_op jit(solution)/shard_map/all_to_all | solution.py:39
  30.6 1.4 add_convert_fusion.1
  32.1 1.3 copy.93
  33.4 7.5 %all-to-all-start.1 = ((bf16[1,128,18,128]{3,2,0,1:T(8,128)(2,1)}), bf16[1,128,18,128]{3,2,0,1:T(8,128)(2,1)S(1)}, u32[]{:S(2)}, u32[]{:S(2)}) async-start(bf16[1,128,18,128]{3,2,0,1:T(8,128)(2,1)} %copy.93), calls=%async_computation.1 | async-start | bytes 1572864 | tf_op jit(solution)/shard_map/all_to_all | solution.py:42
  40.9 0.6 slice_bitcast_fusion.36
  41.5 0.6 slice_bitcast_fusion.8
  42.2 19.2 %all-to-all-done.1 = bf16[1,128,18,128]{3,2,0,1:T(8,128)(2,1)S(1)} async-done(((bf16[1,128,18,128]{3,2,0,1:T(8,128)(2,1)}), bf16[1,128,18,128]{3,2,0,1:T(8,128)(2,1)S(1)}, u32[]{:S(2)}, u32[]{:S(2)}) %all-to-all-start.1) | async-done | bytes 589856 | tf_op jit(solution)/shard_map/all_to_all | solution.py:42
  61.6 0.5 copy.96
  63.4 0.7 maximum_convert_fusion.3
  64.1 0.7 maximum_convert_fusion.2
  64.9 0.8 maximum_convert_fusion.1
  65.7 0.8 maximum_convert_fusion
  66.4 3.2 %fusion.50 = (f32[4,32,18]{1,2,0:T(8,128)S(1)}, f32[1,4,32,18,128]{4,2,3,1,0:T(8,128)}) fusion(f32[128]{0:T(128)S(1)} %get-tuple-element.90, f32[1,4,32,18,128]{4,1,3,2,0:T(4,128)S(1)} %bitcast.177, f32[128]{0:T(128)S(1)} %get-tuple-element.89, f32[1,4,32,18,128]{4,1,3,2,0:T(4,128)S(1)} %bitcast.175, f32[128]{0:T(128)S(1)} %get-tuple-element.88, ...), kind=kLoop, calls=%fused_computation.165 | loop fusion | flops 5601024 | bytes 11220480 | tf_op jit(solution)/shard_map/reduce_sum | solution.py:23
  69.7 2.0 %multiply_reduce_fusion.1 = f32[4,32,18]{1,2,0:T(8,128)S(1)} fusion(f32[1,4,32,18,128]{4,2,3,1,0:T(8,128)} %get-tuple-element.8, f32[4,32,18]{1,2,0:T(8,128)S(1)} %broadcast_multiply_fusion.1), kind=kLoop, calls=%fused_computation.80 | loop fusion | flops 882432 | bytes 1198080 | tf_op jit(solution)/shard_map/reduce_sum | solution.py:25
  72.3 0.9 copy.113
  73.1 10.1 %multiply_convert_fusion.1 = bf16[1,4,576,128]{3,1,2,0:T(4,128)(2,1)S(1)} fusion(bf16[1,4,576,128]{3,1,2,0:T(4,128)(2,1)S(1)} %bitcast.156, f32[128]{0:T(128)S(1)} %copy-done.30, f32[4,576]{0,1:T(8,128)} %copy.113, f32[4,576]{0,1:T(8,128)S(1)} %copy.108, f32[128]{0:T(128)S(1)} %get-tuple-element.90, f32[128]{0:T(128)S(1)} %get-tuple-element.89, ...), kind=kLoop, calls=%fused_computation.79 | loop fusion | flops 11206656 | bytes 5921792 | tf_op jit(solution)/shard_map/convert_element_type | solution.py:26
  83.4 0.8 copy-done.32
  84.2 5.6 %fusion.2 = bf16[2304,256]{1,0:T(8,128)(2,1)S(1)} fusion(bf16[2304,128]{1,0:T(8,128)(2,1)S(1)} %bitcast.194, bf16[2,128,256]{2,1,0:T(8,128)(2,1)S(1)} %copy-done.32), kind=kOutput, calls=%fused_computation.4 | convolution fusion | flops 189333504 | bytes 1835008 | tf_op jit(solution)/shard_map/dot_general | solution.py:29
  89.8 0.5 fusion.23
  90.3 1.3 copy.115
  91.6 7.0 %all-to-all-start.2 = ((bf16[1,4,576,128]{3,1,0,2:T(4,128)(2,1)}), bf16[1,4,576,128]{3,1,0,2:T(4,128)(2,1)S(1)}, u32[]{:S(2)}, u32[]{:S(2)}) async-start(bf16[1,4,576,128]{3,1,0,2:T(4,128)(2,1)} %copy.115), calls=%async_computation.2 | async-start | bytes 1179648 | tf_op jit(solution)/shard_map/all_to_all | solution.py:39
  98.6 15.8 %all-to-all-done.2 = bf16[1,4,576,128]{3,1,0,2:T(4,128)(2,1)S(1)} async-done(((bf16[1,4,576,128]{3,1,0,2:T(4,128)(2,1)}), bf16[1,4,576,128]{3,1,0,2:T(4,128)(2,1)S(1)}, u32[]{:S(2)}, u32[]{:S(2)}) %all-to-all-start.2) | async-done | bytes 589856 | tf_op jit(solution)/shard_map/all_to_all | solution.py:39
  114.7 1.4 add_convert_fusion
  116.2 0.4 copy.117
  116.6 27.1 %all_to_all.72 = bf16[1,128,18,128]{3,2,0,1:T(8,128)(2,1)S(1)} all-to-all(bf16[1,128,18,128]{3,2,0,1:T(8,128)(2,1)S(1)} %copy.117), channel_id=1, replica_groups=mesh['section'=4,'band'=32,'members'=2] {'band'}, dimensions={1} | all-to-all | bytes 1179648 | tf_op jit(solution)/shard_map/all_to_all | solution.py:42
  143.9 0.5 copy.120
  145.8 0.3 maximum_convert_fusion.11
  146.2 0.3 maximum_convert_fusion.12
  146.5 0.3 maximum_convert_fusion.10
  147.3 0.3 maximum_convert_fusion.9
  147.7 0.3 maximum_convert_fusion.14
  148.0 0.3 maximum_convert_fusion.8
  149.1 3.2 %fusion.48 = (f32[4,32,18]{1,2,0:T(8,128)S(1)}, f32[1,4,32,18,128]{4,2,3,1,0:T(8,128)}) fusion(f32[128]{0:T(128)S(1)} %copy-done.22, f32[1,4,32,18,128]{4,1,3,2,0:T(4,128)S(1)} %bitcast.185, f32[128]{0:T(128)S(1)} %copy-done.23, f32[1,4,32,18,128]{4,1,3,2,0:T(4,128)S(1)} %bitcast.183, f32[128]{0:T(128)S(1)} %copy-done.24, ...), kind=kLoop, calls=%fused_computation.164 | loop fusion | flops 5601024 | bytes 11220480 | tf_op jit(solution)/shard_map/reduce_sum | solution.py:23
  152.3 0.6 broadcast_multiply_fusion
  152.9 1.5 copy.131
  154.4 2.0 %multiply_reduce_fusion = f32[4,32,18]{1,2,0:T(8,128)S(1)} fusion(f32[1,4,32,18,128]{4,2,3,1,0:T(8,128)} %get-tuple-element.6, f32[4,32,18]{1,2,0:T(8,128)} %broadcast_multiply_fusion), kind=kLoop, calls=%fused_computation.77 | loop fusion | flops 882432 | bytes 1198080 | tf_op jit(solution)/shard_map/reduce_sum | solution.py:25
  156.4 0.7 add_sqrt_fusion
  157.0 1.5 copy.136
  158.6 1.5 sqrt.25
  160.1 1.5 div.70
  161.7 1.6 copy.132
  163.2 1.6 copy.137
  164.8 7.2 %multiply_convert_fusion = bf16[1,4,576,128]{3,1,2,0:T(4,128)(2,1)S(1)} fusion(bf16[1,4,576,128]{3,1,2,0:T(4,128)(2,1)S(1)} %bitcast.165, f32[128]{0:T(128)} %get-tuple-element.81, f32[4,576]{0,1:T(8,128)} %copy.137, f32[4,576]{0,1:T(8,128)} %copy.132, f32[128]{0:T(128)} %get-tuple-element.42, f32[128]{0:T(128)} %get-tuple-element.43, ...), kind=kLoop, calls=%fused_computation.76 | loop fusion | flops 11206656 | bytes 5921792 | tf_op jit(solution)/shard_map/convert_element_type | solution.py:26
  172.1 0.8 copy-done.33
  172.9 5.4 %fusion.5 = bf16[2304,256]{1,0:T(8,128)(2,1)S(1)} fusion(bf16[2304,128]{1,0:T(8,128)(2,1)S(1)} %bitcast.195, bf16[2,128,256]{2,1,0:T(8,128)(2,1)S(1)} %copy-done.33), kind=kOutput, calls=%fused_computation.7 | convolution fusion | flops 189333504 | bytes 1835008 | tf_op jit(solution)/shard_map/dot_general | solution.py:29
  178.3 1.3 fusion.22
  (101 shorter events, 5.4 us)
Async XLA Ops:
  0.0 14.0 %copy-start.19 = (bf16[2,9,128]{2,0,1:T(2,128)(2,1)S(1)}, bf16[2,9,128]{2,0,1:T(2,128)(2,1)}, u32[]{:S(2)}) copy-start(bf16[2,9,128]{2,0,1:T(2,128)(2,1)} %param.7) | copy-start | bytes 13828
  2.4 28.0 %all-to-all-start = ((bf16[1,4,576,128]{3,1,0,2:T(4,128)(2,1)}), bf16[1,4,576,128]{3,1,0,2:T(4,128)(2,1)S(1)}, u32[]{:S(2)}, u32[]{:S(2)}) async-start(bf16[1,4,576,128]{3,1,0,2:T(4,128)(2,1)} %copy.91), calls=%async_computation | async-start | bytes 1179648 | tf_op jit(solution)/shard_map/all_to_all | solution.py:39
  32.1 8.8 %copy-start.31 = (f32[2,128]{1,0:T(2,128)S(1)}, f32[2,128]{1,0:T(2,128)}, u32[]{:S(2)}) copy-start(f32[2,128]{1,0:T(2,128)} %param.9) | copy-start | bytes 3076
  32.1 9.4 %copy-start.20 = (bf16[2,9,128]{2,0,1:T(2,128)(2,1)S(1)}, bf16[2,9,128]{2,0,1:T(2,128)(2,1)}, u32[]{:S(2)}) copy-start(bf16[2,9,128]{2,0,1:T(2,128)(2,1)} %param.8) | copy-start | bytes 13828
  33.4 28.0 %all-to-all-start.1 = ((bf16[1,128,18,128]{3,2,0,1:T(8,128)(2,1)}), bf16[1,128,18,128]{3,2,0,1:T(8,128)(2,1)S(1)}, u32[]{:S(2)}, u32[]{:S(2)}) async-start(bf16[1,128,18,128]{3,2,0,1:T(8,128)(2,1)} %copy.93), calls=%async_computation.1 | async-start | bytes 1572864 | tf_op jit(solution)/shard_map/all_to_all | solution.py:42
  62.4 3.2 %copy-start.6 = (bf16[1,4,564,128]{3,1,2,0:T(4,128)(2,1)}, bf16[1,4,564,128]{3,1,2,0:T(4,128)(2,1)S(1)}, u32[]{:S(2)}) copy-start(bf16[1,4,564,128]{3,1,2,0:T(4,128)(2,1)S(1)} %get-tuple-element.27) | copy-start | bytes 1732612
  62.5 3.2 %copy-start.7 = (bf16[1,4,564,128]{3,1,2,0:T(4,128)(2,1)}, bf16[1,4,564,128]{3,1,2,0:T(4,128)(2,1)S(1)}, u32[]{:S(2)}) copy-start(bf16[1,4,564,128]{3,1,2,0:T(4,128)(2,1)S(1)} %get-tuple-element.28) | copy-start | bytes 1732612
  62.8 2.1 %copy-start.2 = (bf16[1,4,567,128]{3,1,2,0:T(4,128)(2,1)}, bf16[1,4,567,128]{3,1,2,0:T(4,128)(2,1)S(1)}, u32[]{:S(2)}) copy-start(bf16[1,4,567,128]{3,1,2,0:T(4,128)(2,1)S(1)} %get-tuple-element.31) | copy-start | bytes 1741828
  62.8 2.1 %copy-start.3 = (bf16[1,4,567,128]{3,1,2,0:T(4,128)(2,1)}, bf16[1,4,567,128]{3,1,2,0:T(4,128)(2,1)S(1)}, u32[]{:S(2)}) copy-start(bf16[1,4,567,128]{3,1,2,0:T(4,128)(2,1)S(1)} %get-tuple-element.32) | copy-start | bytes 1741828
  63.1 1.0 copy-start
  69.6 3.5 %copy-start.1 = (bf16[1,4,570,128]{3,1,2,0:T(4,128)(2,1)S(1)}, bf16[1,4,570,128]{3,1,2,0:T(4,128)(2,1)}, u32[]{:S(2)}) copy-start(bf16[1,4,570,128]{3,1,2,0:T(4,128)(2,1)} %copy-done) | copy-start | bytes 1751044
  69.6 3.5 %copy-start.30 = (f32[128]{0:T(128)S(1)}, f32[128]{0:T(128)}, u32[]{:S(2)}) copy-start(f32[128]{0:T(128)} %get-tuple-element.82) | copy-start | bytes 1540
  83.3 0.9 copy-start.32
  84.2 5.7 %copy-start.10 = (bf16[1,4,576,128]{3,2,1,0:T(8,128)(2,1)S(1)}, bf16[1,4,576,128]{3,2,1,0:T(8,128)(2,1)}, u32[]{:S(2)}) copy-start(bf16[1,4,576,128]{3,2,1,0:T(8,128)(2,1)} %param.6) | copy-start | bytes 1769476
  84.2 5.7 %copy-start.11 = (bf16[2,256,128]{2,1,0:T(8,128)(2,1)S(1)}, bf16[2,256,128]{2,1,0:T(8,128)(2,1)}, u32[]{:S(2)}) copy-start(bf16[2,256,128]{2,1,0:T(8,128)(2,1)} %param.11) | copy-start | bytes 393220
  91.6 22.9 %all-to-all-start.2 = ((bf16[1,4,576,128]{3,1,0,2:T(4,128)(2,1)}), bf16[1,4,576,128]{3,1,0,2:T(4,128)(2,1)S(1)}, u32[]{:S(2)}, u32[]{:S(2)}) async-start(bf16[1,4,576,128]{3,1,0,2:T(4,128)(2,1)} %copy.115), calls=%async_computation.2 | async-start | bytes 1179648 | tf_op jit(solution)/shard_map/all_to_all | solution.py:39
  144.4 1.4 copy-start.17
  144.4 1.8 copy-start.18
  144.4 2.1 %copy-start.15 = (bf16[1,4,6,128]{3,1,2,0:T(4,128)(2,1)}, bf16[1,4,6,128]{3,1,2,0:T(4,128)(2,1)S(1)}, u32[]{:S(2)}) copy-start(bf16[1,4,6,128]{3,1,2,0:T(4,128)(2,1)S(1)} %get-tuple-element.17) | copy-start | bytes 18436
  144.4 2.5 %copy-start.16 = (bf16[1,4,6,128]{3,1,2,0:T(4,128)(2,1)}, bf16[1,4,6,128]{3,1,2,0:T(4,128)(2,1)S(1)}, u32[]{:S(2)}) copy-start(bf16[1,4,6,128]{3,1,2,0:T(4,128)(2,1)S(1)} %get-tuple-element.18) | copy-start | bytes 18436
  144.5 2.8 %copy-start.13 = (bf16[1,4,9,128]{3,1,2,0:T(4,128)(2,1)}, bf16[1,4,9,128]{3,1,2,0:T(4,128)(2,1)S(1)}, u32[]{:S(2)}) copy-start(bf16[1,4,9,128]{3,1,2,0:T(4,128)(2,1)S(1)} %get-tuple-element.13) | copy-start | bytes 27652
  144.5 3.2 %copy-start.14 = (bf16[1,4,9,128]{3,1,2,0:T(4,128)(2,1)}, bf16[1,4,9,128]{3,1,2,0:T(4,128)(2,1)S(1)}, u32[]{:S(2)}) copy-start(bf16[1,4,9,128]{3,1,2,0:T(4,128)(2,1)S(1)} %get-tuple-element.14) | copy-start | bytes 27652
  144.8 3.2 %copy-start.8 = (bf16[1,4,564,128]{3,1,2,0:T(4,128)(2,1)}, bf16[1,4,564,128]{3,1,2,0:T(4,128)(2,1)S(1)}, u32[]{:S(2)}) copy-start(bf16[1,4,564,128]{3,1,2,0:T(4,128)(2,1)S(1)} %get-tuple-element.11) | copy-start | bytes 1732612
  144.8 3.6 %copy-start.9 = (bf16[1,4,564,128]{3,1,2,0:T(4,128)(2,1)}, bf16[1,4,564,128]{3,1,2,0:T(4,128)(2,1)S(1)}, u32[]{:S(2)}) copy-start(bf16[1,4,564,128]{3,1,2,0:T(4,128)(2,1)S(1)} %get-tuple-element.12) | copy-start | bytes 1732612
  145.1 2.1 %copy-start.4 = (bf16[1,4,567,128]{3,1,2,0:T(4,128)(2,1)}, bf16[1,4,567,128]{3,1,2,0:T(4,128)(2,1)S(1)}, u32[]{:S(2)}) copy-start(bf16[1,4,567,128]{3,1,2,0:T(4,128)(2,1)S(1)} %get-tuple-element.15) | copy-start | bytes 1741828
  145.2 2.5 %copy-start.5 = (bf16[1,4,567,128]{3,1,2,0:T(4,128)(2,1)}, bf16[1,4,567,128]{3,1,2,0:T(4,128)(2,1)S(1)}, u32[]{:S(2)}) copy-start(bf16[1,4,567,128]{3,1,2,0:T(4,128)(2,1)S(1)} %get-tuple-element.16) | copy-start | bytes 1741828
  148.4 0.6 copy-start.21
  148.4 0.6 copy-start.22
  148.4 0.6 copy-start.23
  148.4 0.7 copy-start.24
  148.4 0.7 copy-start.25
  148.4 0.7 copy-start.26
  148.4 0.7 copy-start.27
  148.4 0.7 copy-start.28
  148.5 0.7 copy-start.29
  172.0 0.9 copy-start.33
  172.9 5.4 %copy-start.12 = (bf16[2,256,128]{2,1,0:T(8,128)(2,1)S(1)}, bf16[2,256,128]{2,1,0:T(8,128)(2,1)}, u32[]{:S(2)}) copy-start(bf16[2,256,128]{2,1,0:T(8,128)(2,1)} %param.11) | copy-start | bytes 393220
where the time goes:
time: 183 us; the launch traced here: 180 us
  waiting for transfers between devices  51.4 us (28%)
  other arithmetic  37.5 us (20%)
  blocking collectives  27.1 us (15%)
  starting transfers between devices  26.1 us (14%)
  local copies, waits for them, and re-layouts  23.9 us (13%)
  matrix products  12.8 us (7%)
    all_to_all x2, waiting for transfers between devices, shards(): lax.all_to_all(state, 'band', split_axis=2, concat_axis=1, tiled=True)  32.2 us
    all_to_all x1, blocking collectives, shards(): lax.all_to_all(mixed, 'band', split_axis=1, concat_axis=2, tiled=True)  27.1 us
    all_to_all x1, waiting for transfers between devices, shards(): lax.all_to_all(mixed, 'band', split_axis=1, concat_axis=2, tiled=True)  19.2 us
    all_to_all x2, starting transfers between devices, shards(): lax.all_to_all(state, 'band', split_axis=2, concat_axis=1, tiled=True)  18.6 us
    convert_element_type x2, other arithmetic, layer_rest(): normed = (centred / jnp.sqrt(var + 1e-06) * gain).astype(jnp.bfloat16)  17.3 us
    dot_general x2, matrix products, layer_rest(): jnp.dot(flat, proj_in, preferred_element_type=jnp.float32)  11.1 us
    all_to_all x1, starting transfers between devices, shards(): lax.all_to_all(mixed, 'band', split_axis=1, concat_axis=2, tiled=True)  7.5 us
    reduce_sum x2, other arithmetic, layer_rest(): mean = jnp.mean(lonmix, axis=-1, keepdims=True)  6.35 us
  transfers between devices with their start and end apart: 3, of which 3 were waited for; matrix products, arithmetic and copies ran while one was open for 1% of the time, Pallas kernels for 0%

commit v1 on v0

v1 whole, which is shorter than its diff:
```python
import functools

import jax
import jax.numpy as jnp
from jax import lax
from jax.experimental import pallas as pl
from jax.experimental.pallas import tpu as pltpu
from jax.sharding import PartitionSpec as P

LAYERS = 2
TAPS = 9
REACH = 12
ROWS = 4
LON = 576
C = 128
H = 256
W = 48
N = LON // W
BANDS = 32
PAD = 16
MESH = pl.DeviceIdType.MESH


def kernel(fields, lat_taps, lon_taps, gains, w_in, w_out, out,
           state0, state1, mixed, result, lat16, lon16, lat32, lon32, gain32, win, wout,
           send_sem, recv_sem, load_sem, out_sem):
    band = lax.axis_index("band")
    has_up = band > 0
    has_down = band < BANDS - 1
    states = (state0, state1)

    barrier = pltpu.get_barrier_semaphore()

    @pl.when(has_up)
    def _():
        pl.semaphore_signal(barrier, inc=1, device_id={"band": band - 1}, device_id_type=MESH)

    @pl.when(has_down)
    def _():
        pl.semaphore_signal(barrier, inc=1, device_id={"band": band + 1}, device_id_type=MESH)

    loads = [
        pltpu.make_async_copy(fields.at[0], state0.at[ROWS:2 * ROWS, 0:LON], load_sem.at[0]),
        pltpu.make_async_copy(fields.at[0, :, 0:16], state0.at[ROWS:2 * ROWS, LON:LON + 16], load_sem.at[1]),
        pltpu.make_async_copy(lat_taps, lat16, load_sem.at[2]),
        pltpu.make_async_copy(lon_taps, lon16, load_sem.at[3]),
        pltpu.make_async_copy(gains, gain32, load_sem.at[4]),
        pltpu.make_async_copy(w_in, win, load_sem.at[5]),
        pltpu.make_async_copy(w_out, wout, load_sem.at[6]),
    ]
    for load in loads:
        load.start()

    def copy(layer, side, piece, start, width):
        place = states[layer]
        if layer == 0:
            source = fields.at[0, :, pl.ds(start, width)]
        else:
            source = place.at[ROWS:2 * ROWS, pl.ds(start, width)]
        first = 2 * ROWS if side == 0 else 0
        return pltpu.make_async_remote_copy(
            src_ref=source,
            dst_ref=place.at[first:first + ROWS, pl.ds(start, width)],
            send_sem=send_sem.at[layer, side, piece],
            recv_sem=recv_sem.at[layer, side, piece],
            device_id={"band": band - 1 if side == 0 else band + 1},
            device_id_type=MESH,
        )

    def send(layer, piece, start, width):
        @pl.when(has_up)
        def _():
            copy(layer, 0, piece, start, width).start()

        @pl.when(has_down)
        def _():
            copy(layer, 1, piece, start, width).start()

    def arrived(layer, piece, start, width):
        @pl.when(has_down)
        def _():
            copy(layer, 0, piece, start, width).wait_recv()

        @pl.when(has_up)
        def _():
            copy(layer, 1, piece, start, width).wait_recv()

    def sent(layer, piece, start, width):
        @pl.when(has_up)
        def _():
            copy(layer, 0, piece, start, width).wait_send()

        @pl.when(has_down)
        def _():
            copy(layer, 1, piece, start, width).wait_send()

    pl.semaphore_wait(barrier, has_up.astype(jnp.int32) + has_down.astype(jnp.int32))

    for piece in range(N):
        send(0, piece, piece * W, W)

    @pl.when(band == 0)
    def _():
        for place in states:
            place[0:ROWS] = jnp.zeros((ROWS,) + place.shape[1:], place.dtype)

    @pl.when(band == BANDS - 1)
    def _():
        for place in states:
            place[2 * ROWS:] = jnp.zeros((ROWS,) + place.shape[1:], place.dtype)

    for load in loads:
        load.wait()
    lat32[...] = lat16[...].astype(jnp.float32)
    lon32[...] = lon16[...].astype(jnp.float32)

    def latmix(layer, start, width):
        place = states[layer]
        for at in range(0, width, 16):
            rows = [place[r, pl.ds(start + at, 16), :].astype(jnp.float32) for r in range(3 * ROWS)]
            for i in range(ROWS):
                total = rows[i] * lat32[0, layer:layer + 1, :]
                for k in range(1, TAPS):
                    total = total + rows[i + k] * lat32[k, layer:layer + 1, :]
                mixed[layer, i, pl.ds(PAD + start + at, 16), :] = total.astype(jnp.bfloat16).astype(jnp.float32)

    def rest(layer, start, width, store, held=None):
        held = start if held is None else held
        for i in range(ROWS):
            total = mixed[layer, i, pl.ds(PAD + start - REACH, width), :] * lon32[0, layer:layer + 1, :]
            for k in range(1, TAPS):
                total = total + mixed[layer, i, pl.ds(PAD + start - REACH + 3 * k, width), :] * lon32[k, layer:layer + 1, :]
            mean = jnp.mean(total, axis=-1, keepdims=True)
            centred = total - mean
            var = jnp.mean(centred * centred, axis=-1, keepdims=True)
            normed = (centred * lax.rsqrt(var + 1e-06) * gain32[layer:layer + 1, :]).astype(jnp.bfloat16)
            inner = jnp.dot(normed, win[layer], preferred_element_type=jnp.float32)
            hidden = (0.5 * inner * (1.0 + lax.erf(inner * 0.7071067811865476))).astype(jnp.bfloat16)
            delta = jnp.dot(hidden, wout[layer], preferred_element_type=jnp.float32)
            old = states[layer][ROWS + i, pl.ds(held, width), :].astype(jnp.float32)
            store(i, (old + delta).astype(jnp.bfloat16))

    def keep(start, width):
        def store(i, value):
            state1[ROWS + i, pl.ds(start, width), :] = value
        return store

    def finish(start, width):
        def store(i, value):
            result[i, pl.ds(start, width), :] = value
        return store

    arrived(0, 0, 0, W)
    latmix(0, 0, W)
    for i in range(ROWS):
        mixed[0, i, PAD + LON:PAD + LON + W, :] = mixed[0, i, PAD:PAD + W, :]
    rest(0, 16, W - 32, keep(16, W - 32))
    send(1, 0, 16, W - 32)

    @pl.loop(1, N)
    def _(piece):
        start = pl.multiple_of(piece * W, 16)
        arrived(0, piece, start, W)
        latmix(0, start, W)
        rest(0, start - 16, W, keep(start - 16, W))
        send(1, piece, start - 16, W)

    rest(0, LON - 16, 32, keep(LON - 16, 32))
    send(1, N, LON - 16, 32)

    arrived(1, 0, 16, W - 32)
    latmix(1, 16, W - 32)

    @pl.loop(1, N)
    def _(piece):
        start = pl.multiple_of(piece * W, 16)
        arrived(1, piece, start - 16, W)
        latmix(1, start - 16, W)

        @pl.when(piece == 1)
        def _():
            for i in range(ROWS):
                mixed[1, i, PAD + LON + 16:PAD + LON + 48, :] = mixed[1, i, PAD + 16:PAD + 48, :]

        rest(1, start - 32, W, finish(start - 32, W))

    arrived(1, N, LON - 16, 32)
    latmix(1, LON - 16, 32)
    rest(1, LON - 32, 32, finish(LON - 32, 32))
    rest(1, LON, 16, finish(0, 16))
    rest(1, LON + 16, 16, finish(16, 16), held=16)

    written = pltpu.make_async_copy(result, out.at[0], out_sem)
    written.start()
    for piece in range(N):
        sent(0, piece, piece * W, W)
    sent(1, 0, 16, W - 32)
    for piece in range(1, N):
        sent(1, piece, piece * W - 16, W)
    sent(1, N, LON - 16, 32)
    written.wait()


def shards(fields, lat_taps, lon_taps, gains, w_in, w_out):
    return pl.pallas_call(
        kernel,
        out_shape=jax.ShapeDtypeStruct(fields.shape, fields.dtype),
        in_specs=[pl.BlockSpec(memory_space=pl.ANY)] * 6,
        out_specs=pl.BlockSpec(memory_space=pl.ANY),
        scratch_shapes=[
            pltpu.VMEM((3 * ROWS, LON + 16, C), jnp.bfloat16),
            pltpu.VMEM((3 * ROWS, LON + 16, C), jnp.bfloat16),
            pltpu.VMEM((LAYERS, ROWS, PAD + LON + 64, C), jnp.float32),
            pltpu.VMEM((ROWS, LON, C), jnp.bfloat16),
            pltpu.VMEM((TAPS, LAYERS, C), jnp.bfloat16),
            pltpu.VMEM((TAPS, LAYERS, C), jnp.bfloat16),
            pltpu.VMEM((TAPS, LAYERS, C), jnp.float32),
            pltpu.VMEM((TAPS, LAYERS, C), jnp.float32),
            pltpu.VMEM((LAYERS, C), jnp.float32),
            pltpu.VMEM((LAYERS, C, H), jnp.bfloat16),
            pltpu.VMEM((LAYERS, H, C), jnp.bfloat16),
            pltpu.SemaphoreType.DMA((LAYERS, 2, N + 1)),
            pltpu.SemaphoreType.DMA((LAYERS, 2, N + 1)),
            pltpu.SemaphoreType.DMA((7,)),
            pltpu.SemaphoreType.DMA,
        ],
        compiler_params=pltpu.CompilerParams(collective_id=0, has_side_effects=True),
        name="step",
    )(fields, jnp.transpose(lat_taps, (1, 0, 2)), jnp.transpose(lon_taps, (1, 0, 2)), gains, w_in, w_out)


def solution(mesh):
    return jax.shard_map(
        shards,
        mesh=mesh,
        in_specs=(P(("members", "section"), "band", None, None), P(), P(), P(), P(), P()),
        out_specs=P(("members", "section"), "band", None, None),
        check_vma=False,
    )
```

time: 183 us -> 38 us (0.21); the launches traced: 180 us -> 37.8 us
  waiting for transfers between devices: 51.4 us -> 0 us
  other arithmetic: 37.5 us -> 0 us
  Pallas kernels: 0 us -> 35.9 us
  blocking collectives: 27.1 us -> 0 us
  starting transfers between devices: 26.1 us -> 0 us
  local copies, waits for them, and re-layouts: 23.9 us -> 1.92 us
  matrix products: 12.8 us -> 0 us
    all_to_all x3 -> x0, waiting for transfers between devices: 51.4 us -> none  [the longest x2 32.2 us: shards(): lax.all_to_all(state, 'band', split_axis=2, concat_axis=1, tiled=True)]
    pallas_call x0 -> x1, Pallas kernels: none -> 35.9 us  [shards(): pl.pallas_call(kernel, out_shape=jax.ShapeDtypeStruct(fields.shape, field...]
    all_to_all x1 -> x0, blocking collectives: 27.1 us -> none  [shards(): lax.all_to_all(mixed, 'band', split_axis=1, concat_axis=2, tiled=True)]
    all_to_all x3 -> x0, starting transfers between devices: 26.1 us -> none  [the longest x2 18.6 us: shards(): lax.all_to_all(state, 'band', split_axis=2, concat_axis=1, tiled=True)]
    convert_element_type x18 -> x0, other arithmetic: 25.9 us -> none  [the longest x2 17.3 us: layer_rest(): normed = (centred / jnp.sqrt(var + 1e-06) * gain).astype(jnp.bfloat16)]
    dot_general x4 -> x0, matrix products: 12.8 us -> none  [the longest x2 11.1 us: layer_rest(): jnp.dot(flat, proj_in, preferred_element_type=jnp.float32)]
    reduce_sum x4 -> x0, other arithmetic: 10.3 us -> none  [the longest x2 6.35 us: layer_rest(): mean = jnp.mean(lonmix, axis=-1, keepdims=True)]
    sqrt x6 -> x0, local copies, waits for them, and re-layouts: 5.75 us -> none  [layer_rest(): normed = (centred / jnp.sqrt(var + 1e-06) * gain).astype(jnp.bfloat16)]
  transfers between devices with their start and end apart: 3 -> 0, of which waited for: 3 -> 0; matrix products, arithmetic and copies ran while one was open for 1% -> 0% of each run, Pallas kernels for 0% -> 0%
where the time goes in v1:
time: 38 us; the launch traced here: 37.8 us
  Pallas kernels  35.9 us (94%)
  local copies, waits for them, and re-layouts  1.92 us (5%)
    pallas_call x1, Pallas kernels, shards(): pl.pallas_call(kernel, out_shape=jax.ShapeDtypeStruct(fields.shape, field...  35.9 us
    unnamed x1, local copies, waits for them, and re-layouts  1.92 us

profile of v1, /device:TPU:6, one launch (start us, length us, event | category | flops | bytes accessed | tf_op | source)
XLA Modules:
  0.0 37.8 jit_solution(265848266099558448)
XLA Ops:
  0.0 35.9 %step.1 = bf16[1,4,576,128]{3,2,1,0:T(8,128)(2,1)} custom-call(bf16[1,4,576,128]{3,2,1,0:T(8,128)(2,1)} %fields.1, bf16[9,2,128]{2,1,0:T(2,128)(2,1)} %bitcast.2, bf16[9,2,128]{2,1,0:T(2,128)(2,1)} %bitcast.3, f32[2,128]{1,0:T(2,128)} %gains.1, bf16[2,128,256]{2,1,0:T(8,128)(2,1)} %w_in.1, bf16[2,256,128]{2,1,0:T(8,128)(2,1)} %w_out.1), custom_call_target="tpu_custom_call" | custom-call | tf_op jit(solution)/shard_map/step/pallas_call | solution.py:205
  35.9 1.9 %copy.8 = bf16[1,4,576,128]{3,2,1,0:T(8,128)(2,1)} copy(bf16[1,4,576,128]{3,2,1,0:T(8,128)(2,1)} %step.1) | data formatting | bytes 1179648

commit v2 on v0

v2 whole, which is shorter than its diff:
```python
import jax
import jax.numpy as jnp
from jax import lax
from jax.experimental import pallas as pl
from jax.experimental.pallas import tpu as pltpu
from jax.sharding import PartitionSpec as P

LAYERS = 2
TAPS = 9
REACH = 12
ROWS = 4
LON = 576
C = 128
H = 256
BANDS = 32
RUN = 8
PAD = 16
BLOCK = 48
MESH = pl.DeviceIdType.MESH

SENT = (
    ((0, 96), (96, 96), (192, 96), (288, 96), (384, 96), (480, 96)),
    ((16, 64), (80, 96), (176, 96), (272, 96), (368, 96), (464, 48), (512, 48), (560, 32)),
)
DONE = (
    ((16, 64), (80, 96), (176, 96), (272, 96), (368, 96), (464, 96)),
    ((32, 32), (64, 96), (160, 96), (256, 96), (352, 96), (448, 48), (496, 48), (544, 64)),
)
NEXT = ((0,), (1,), (2,), (3,), (4,), (5, 6))


def kernel(fields, lat_taps, lon_taps, gains, w_in, w_out, out,
           state0, state1, mixed, lat16, lon16, lat32, lon32, gain32, win, wout,
           send_sem, recv0_sem, recv1_sem, load_sem, ready_sem):
    band = lax.axis_index("band")
    place_in_run = lax.rem(band, RUN)
    opens = place_in_run == 0
    closes = place_in_run == RUN - 1
    has_up = band > 0
    has_down = band < BANDS - 1
    inside = jnp.logical_and(has_up, has_down)
    up_by_barrier = jnp.logical_and(has_up, jnp.logical_not(opens))
    up_by_ready = jnp.logical_and(has_up, opens)
    down_by_barrier = jnp.logical_and(has_down, closes)
    down_by_ready = jnp.logical_and(has_down, jnp.logical_not(closes))
    states = (state0, state1)
    recv_sems = (recv0_sem, recv1_sem)
    above, below = {"band": band - 1}, {"band": band + 1}

    barrier = pltpu.get_barrier_semaphore()

    @pl.when(down_by_ready)
    def _():
        pl.semaphore_signal(barrier, inc=1, device_id=below, device_id_type=MESH)

    @pl.when(up_by_ready)
    def _():
        pl.semaphore_signal(barrier, inc=1, device_id=above, device_id_type=MESH)

    own = pltpu.make_async_copy(fields.at[0], state0.at[ROWS:2 * ROWS, 0:LON], load_sem.at[0])
    loads = [
        pltpu.make_async_copy(lat_taps, lat16, load_sem.at[1]),
        pltpu.make_async_copy(lon_taps, lon16, load_sem.at[2]),
        pltpu.make_async_copy(gains, gain32, load_sem.at[3]),
        pltpu.make_async_copy(w_in, win, load_sem.at[4]),
        pltpu.make_async_copy(w_out, wout, load_sem.at[5]),
    ]
    own.start()
    for load in loads:
        load.start()

    def copy(layer, side, piece, sending=True):
        place = states[layer]
        start, width = SENT[layer][piece]
        first = 2 * ROWS if side == 0 else 0
        source = fields.at[0, :, start:start + width] if layer == 0 else place.at[ROWS:2 * ROWS, start:start + width]
        return pltpu.make_async_remote_copy(
            src_ref=source,
            dst_ref=place.at[first:first + ROWS, start:start + width],
            send_sem=send_sem.at[layer, side],
            recv_sem=recv_sems[layer].at[piece],
            device_id=above if side == 0 else below,
            device_id_type=MESH,
        )

    def send_side(layer, side, pieces):
        for piece in pieces:
            copy(layer, side, piece).start()

    def send(layer, pieces):
        @pl.when(has_up)
        def _():
            send_side(layer, 0, pieces)

        @pl.when(has_down)
        def _():
            send_side(layer, 1, pieces)

    def awaited(layer, piece, rows):
        start, width = SENT[layer][piece]
        part = states[layer].at[0:rows, start:start + width]
        return pltpu.make_async_remote_copy(
            src_ref=part, dst_ref=part, send_sem=send_sem.at[0, 0], recv_sem=recv_sems[layer].at[piece],
            device_id=above, device_id_type=MESH,
        )

    def arrived(layer, piece):
        @pl.when(inside)
        def _():
            awaited(layer, piece, 2 * ROWS).wait_recv()

        @pl.when(jnp.logical_not(inside))
        def _():
            awaited(layer, piece, ROWS).wait_recv()

    def sent(layer, side):
        start = SENT[layer][0][0]
        part = states[layer].at[0:ROWS, start:start + LON]
        pltpu.make_async_remote_copy(
            src_ref=part, dst_ref=part, send_sem=send_sem.at[layer, side], recv_sem=recv0_sem.at[0],
            device_id=above, device_id_type=MESH,
        ).wait_send()

    all_first = range(len(SENT[0]))

    @pl.when(jnp.logical_or(up_by_barrier, down_by_barrier))
    def _():
        pl.semaphore_wait(barrier, up_by_barrier.astype(jnp.int32) + down_by_barrier.astype(jnp.int32))

    @pl.when(up_by_barrier)
    def _():
        pl.semaphore_signal(ready_sem.at[0], inc=1, device_id=above, device_id_type=MESH)
        send_side(0, 0, all_first)

    @pl.when(down_by_barrier)
    def _():
        pl.semaphore_signal(ready_sem.at[1], inc=1, device_id=below, device_id_type=MESH)
        send_side(0, 1, all_first)

    @pl.when(down_by_ready)
    def _():
        pl.semaphore_wait(ready_sem.at[0], 1)
        send_side(0, 1, all_first)

    @pl.when(up_by_ready)
    def _():
        pl.semaphore_wait(ready_sem.at[1], 1)
        send_side(0, 0, all_first)

    @pl.when(jnp.logical_not(has_up))
    def _():
        for place in states:
            place[0:ROWS] = jnp.zeros((ROWS,) + place.shape[1:], place.dtype)

    @pl.when(jnp.logical_not(has_down))
    def _():
        for place in states:
            place[2 * ROWS:] = jnp.zeros((ROWS,) + place.shape[1:], place.dtype)

    own.wait()
    for load in loads:
        load.wait()
    state0[ROWS:2 * ROWS, LON:LON + 16, :] = state0[ROWS:2 * ROWS, 0:16, :]
    lat32[...] = lat16[...].astype(jnp.float32)
    lon32[...] = lon16[...].astype(jnp.float32)

    def latmix(layer, piece):
        place = states[layer]
        start, width = SENT[layer][piece]
        for at in range(start, start + width, 16):
            rows = [place[r, at:at + 16, :].astype(jnp.float32) for r in range(3 * ROWS)]
            for i in range(ROWS):
                total = rows[i] * lat32[0, layer:layer + 1, :]
                for k in range(1, TAPS):
                    total = total + rows[i + k] * lat32[k, layer:layer + 1, :]
                total = total.astype(jnp.bfloat16).astype(jnp.float32)
                mixed[layer, i, PAD + at:PAD + at + 16, :] = total
                if at + LON < (LAYERS + 1) * 16 + LON + layer * 16 - 16:
                    mixed[layer, i, PAD + at + LON:PAD + at + LON + 16, :] = total

    def rest(layer, start, width, store):
        totals = []
        for i in range(ROWS):
            at = PAD + start - REACH
            total = mixed[layer, i, at:at + width, :] * lon32[0, layer:layer + 1, :]
            for k in range(1, TAPS):
                total = total + mixed[layer, i, at + 3 * k:at + 3 * k + width, :] * lon32[k, layer:layer + 1, :]
            totals.append(total)
        total = jnp.concatenate(totals, axis=0)
        mean = jnp.mean(total, axis=-1, keepdims=True)
        centred = total - mean
        var = jnp.mean(centred * centred, axis=-1, keepdims=True)
        normed = (centred * lax.rsqrt(var + 1e-06) * gain32[layer:layer + 1, :]).astype(jnp.bfloat16)
        inner = jnp.dot(normed, win[layer], preferred_element_type=jnp.float32)
        hidden = (0.5 * inner * (1.0 + lax.erf(inner * 0.7071067811865476))).astype(jnp.bfloat16)
        delta = jnp.dot(hidden, wout[layer], preferred_element_type=jnp.float32)
        for i in range(ROWS):
            old = states[layer][ROWS + i, start:start + width, :].astype(jnp.float32)
            store(i, start, width, (old + delta[i * width:(i + 1) * width]).astype(jnp.bfloat16))

    def keep(i, start, width, value):
        state1[ROWS + i, start:start + width, :] = value
        if start == 16:
            state1[ROWS + i, LON + 16:LON + 32, :] = value[:16]

    def finish(i, start, width, value):
        if start + width <= LON:
            out[0, i, start:start + width, :] = value
        else:
            out[0, i, start:LON, :] = value[:LON - start]
            out[0, i, 0:start + width - LON, :] = value[LON - start:]

    def run(layer, start, width, store):
        for at in range(start, start + width, BLOCK):
            rest(layer, at, min(BLOCK, start + width - at), store)

    for piece in range(len(SENT[0])):
        arrived(0, piece)
        latmix(0, piece)
        run(0, *DONE[0][piece], keep)
        send(1, NEXT[piece])
    run(0, LON - 16, 32, keep)
    send(1, (len(SENT[1]) - 1,))

    for piece in range(len(SENT[1])):
        arrived(1, piece)
        latmix(1, piece)
        if piece < len(SENT[1]) - 1:
            run(1, *DONE[1][piece], finish)
        else:
            rest(1, *DONE[1][piece], finish)

    for layer in range(LAYERS):
        @pl.when(has_up)
        def _():
            sent(layer, 0)

        @pl.when(has_down)
        def _():
            sent(layer, 1)


def shards(fields, lat_taps, lon_taps, gains, w_in, w_out):
    return pl.pallas_call(
        kernel,
        out_shape=pltpu.VMEM(fields.shape, fields.dtype),
        in_specs=[pl.BlockSpec(memory_space=pl.ANY)] * 6,
        out_specs=pl.BlockSpec(memory_space=pltpu.VMEM),
        scratch_shapes=[
            pltpu.VMEM((3 * ROWS, LON + 32, C), jnp.bfloat16),
            pltpu.VMEM((3 * ROWS, LON + 32, C), jnp.bfloat16),
            pltpu.VMEM((LAYERS, ROWS, PAD + LON + 64, C), jnp.float32),
            pltpu.VMEM((TAPS, LAYERS, C), jnp.bfloat16),
            pltpu.VMEM((TAPS, LAYERS, C), jnp.bfloat16),
            pltpu.VMEM((TAPS, LAYERS, C), jnp.float32),
            pltpu.VMEM((TAPS, LAYERS, C), jnp.float32),
            pltpu.VMEM((LAYERS, C), jnp.float32),
            pltpu.VMEM((LAYERS, C, H), jnp.bfloat16),
            pltpu.VMEM((LAYERS, H, C), jnp.bfloat16),
            pltpu.SemaphoreType.DMA((LAYERS, 2)),
            pltpu.SemaphoreType.DMA((len(SENT[0]),)),
            pltpu.SemaphoreType.DMA((len(SENT[1]),)),
            pltpu.SemaphoreType.DMA((6,)),
            pltpu.SemaphoreType.REGULAR((2,)),
        ],
        compiler_params=pltpu.CompilerParams(collective_id=0, has_side_effects=True),
        name="step",
    )(fields, jnp.transpose(lat_taps, (1, 0, 2)), jnp.transpose(lon_taps, (1, 0, 2)), gains, w_in, w_out)


def solution(mesh):
    return jax.shard_map(
        shards,
        mesh=mesh,
        in_specs=(P(("members", "section"), "band", None, None), P(), P(), P(), P(), P()),
        out_specs=P(("members", "section"), "band", None, None),
        check_vma=False,
    )
```

time: 183 us -> 35.1 us (0.19); the launches traced: 180 us -> 35 us
  waiting for transfers between devices: 51.4 us -> 0 us
  other arithmetic: 37.5 us -> 0 us
  Pallas kernels: 0 us -> 34.2 us
  blocking collectives: 27.1 us -> 0 us
  starting transfers between devices: 26.1 us -> 0 us
  local copies, waits for them, and re-layouts: 23.9 us -> 0.82 us
  matrix products: 12.8 us -> 0 us
    all_to_all x3 -> x0, waiting for transfers between devices: 51.4 us -> none  [the longest x2 32.2 us: shards(): lax.all_to_all(state, 'band', split_axis=2, concat_axis=1, tiled=True)]
    pallas_call x0 -> x1, Pallas kernels: none -> 34.2 us  [shards(): pl.pallas_call(kernel, out_shape=pltpu.VMEM(fields.shape, fields.dtype),...]
    all_to_all x1 -> x0, blocking collectives: 27.1 us -> none  [shards(): lax.all_to_all(mixed, 'band', split_axis=1, concat_axis=2, tiled=True)]
    all_to_all x3 -> x0, starting transfers between devices: 26.1 us -> none  [the longest x2 18.6 us: shards(): lax.all_to_all(state, 'band', split_axis=2, concat_axis=1, tiled=True)]
    convert_element_type x18 -> x0, other arithmetic: 25.9 us -> none  [the longest x2 17.3 us: layer_rest(): normed = (centred / jnp.sqrt(var + 1e-06) * gain).astype(jnp.bfloat16)]
    dot_general x4 -> x0, matrix products: 12.8 us -> none  [the longest x2 11.1 us: layer_rest(): jnp.dot(flat, proj_in, preferred_element_type=jnp.float32)]
    reduce_sum x4 -> x0, other arithmetic: 10.3 us -> none  [the longest x2 6.35 us: layer_rest(): mean = jnp.mean(lonmix, axis=-1, keepdims=True)]
    sqrt x6 -> x0, local copies, waits for them, and re-layouts: 5.75 us -> none  [layer_rest(): normed = (centred / jnp.sqrt(var + 1e-06) * gain).astype(jnp.bfloat16)]
  transfers between devices with their start and end apart: 3 -> 0, of which waited for: 3 -> 0; matrix products, arithmetic and copies ran while one was open for 1% -> 0% of each run, Pallas kernels for 0% -> 0%
where the time goes in v2:
time: 35.1 us; the launch traced here: 35 us
  Pallas kernels  34.2 us (97%)
  local copies, waits for them, and re-layouts  0.82 us (2%)
    pallas_call x1, Pallas kernels, shards(): pl.pallas_call(kernel, out_shape=pltpu.VMEM(fields.shape, fields.dtype),...  34.2 us
    unnamed x1, local copies, waits for them, and re-layouts  0.82 us

profile of v2, /device:TPU:6, one launch (start us, length us, event | category | flops | bytes accessed | tf_op | source)
XLA Modules:
  0.0 35.0 jit_solution(3480936670820666207)
XLA Ops:
  0.0 34.2 %step.1 = bf16[1,4,576,128]{3,2,1,0:T(8,128)(2,1)S(1)} custom-call(bf16[1,4,576,128]{3,2,1,0:T(8,128)(2,1)} %fields.1, bf16[9,2,128]{2,1,0:T(2,128)(2,1)} %bitcast.2, bf16[9,2,128]{2,1,0:T(2,128)(2,1)} %bitcast.3, f32[2,128]{1,0:T(2,128)} %gains.1, bf16[2,128,256]{2,1,0:T(8,128)(2,1)} %w_in.1, bf16[2,256,128]{2,1,0:T(8,128)(2,1)} %w_out.1), custom_call_target="tpu_custom_call" | custom-call | tf_op jit(solution)/shard_map/step/pallas_call | solution.py:244
  34.2 0.8 %copy.8 = bf16[1,4,576,128]{3,2,1,0:T(8,128)(2,1)} copy(bf16[1,4,576,128]{3,2,1,0:T(8,128)(2,1)S(1)} %step.1) | data formatting | bytes 1179648

commit v3 on v2

--- a/solution.py
+++ b/solution.py
@@ -26,14 +26,16 @@
     ((16, 64), (80, 96), (176, 96), (272, 96), (368, 96), (464, 96)),
     ((32, 32), (64, 96), (160, 96), (256, 96), (352, 96), (448, 48), (496, 48), (544, 64)),
 )
+RELAYED = ((3, 4, 5), (0, 1, 2))
 NEXT = ((0,), (1,), (2,), (3,), (4,), (5, 6))
 
 
 def kernel(fields, lat_taps, lon_taps, gains, w_in, w_out, out,
            state0, state1, mixed, lat16, lon16, lat32, lon32, gain32, win, wout,
-           send_sem, recv0_sem, recv1_sem, load_sem, ready_sem):
+           relay0, relay1, send_sem, recv0_sem, recv1_sem, load_sem, ready_sem, relay_sem):
     band = lax.axis_index("band")
     place_in_run = lax.rem(band, RUN)
+    run_index = band // RUN
     opens = place_in_run == 0
     closes = place_in_run == RUN - 1
     has_up = band > 0
@@ -46,6 +48,23 @@
     states = (state0, state1)
     recv_sems = (recv0_sem, recv1_sem)
     above, below = {"band": band - 1}, {"band": band + 1}
+    run_before, run_after = {"band": band - RUN}, {"band": band + RUN}
+    run_start, run_end = {"band": band - (RUN - 1)}, {"band": band + (RUN - 1)}
+    relays = (relay0, relay1)
+    later, sooner = run_index > 0, run_index < BANDS // RUN - 1
+    by_run_after = jnp.logical_and(closes, sooner)
+    by_run_before = jnp.logical_and(opens, later)
+    passes_down = jnp.logical_and(closes, later)
+    passes_up = jnp.logical_and(opens, sooner)
+
+    def down_count(run):
+        return run + 1
+
+    def up_count(run):
+        return BANDS // RUN - run
+
+    def is_relayed(layer, slot, count):
+        return count >= (len(RELAYED[0]) - slot if layer == 0 else slot + 1)
 
     barrier = pltpu.get_barrier_semaphore()
 
@@ -56,6 +75,14 @@
     @pl.when(up_by_ready)
     def _():
         pl.semaphore_signal(barrier, inc=1, device_id=above, device_id_type=MESH)
+
+    @pl.when(opens)
+    def _():
+        pl.semaphore_signal(barrier, inc=1, device_id=run_end, device_id_type=MESH)
+
+    @pl.when(jnp.logical_and(sooner, jnp.logical_or(opens, closes)))
+    def _():
+        pl.semaphore_signal(barrier, inc=1, device_id=run_after, device_id_type=MESH)
 
     own = pltpu.make_async_copy(fields.at[0], state0.at[ROWS:2 * ROWS, 0:LON], load_sem.at[0])
     loads = [
@@ -83,18 +110,91 @@
             device_id_type=MESH,
         )
 
-    def send_side(layer, side, pieces):
+    def slot_of(layer, piece):
+        return layer * len(RELAYED[0]) + RELAYED[layer].index(piece)
+
+    def detour(layer, side, piece):
+        start, width = SENT[layer][piece]
+        source = fields.at[0, :, start:start + width] if layer == 0 else state1.at[ROWS:2 * ROWS, start:start + width]
+        return pltpu.make_async_remote_copy(
+            src_ref=source,
+            dst_ref=relays[layer].at[:, start:start + width],
+            send_sem=send_sem.at[layer, side],
+            recv_sem=relay_sem.at[slot_of(layer, piece)],
+            device_id=run_before if side == 0 else run_after,
+            device_id_type=MESH,
+        )
+
+    def onward(layer, side, piece):
+        start, width = SENT[layer][piece]
+        first = 2 * ROWS if side == 0 else 0
+        return pltpu.make_async_remote_copy(
+            src_ref=relays[layer].at[:, start:start + width],
+            dst_ref=states[layer].at[first:first + ROWS, start:start + width],
+            send_sem=relay_sem.at[slot_of(layer, piece)],
+            recv_sem=recv_sems[layer].at[piece],
+            device_id=run_end if side == 0 else run_start,
+            device_id_type=MESH,
+        )
+
+    def goes_round(layer, side, piece):
+        if piece not in RELAYED[layer] or (layer == 1 and side == 0):
+            return None
+        slot = RELAYED[layer].index(piece)
+        if side == 0:
+            return jnp.logical_and(by_run_before, is_relayed(layer, slot, up_count(run_index)))
+        return jnp.logical_and(by_run_after, is_relayed(layer, slot, down_count(run_index)))
+
+    def send_direct(layer, side, pieces):
         for piece in pieces:
-            copy(layer, side, piece).start()
+            round_about = goes_round(layer, side, piece)
+            if round_about is None:
+                copy(layer, side, piece).start()
+            else:
+                @pl.when(jnp.logical_not(round_about))
+                def _():
+                    copy(layer, side, piece).start()
+
+    def send_round(layer, side, pieces):
+        for piece in pieces:
+            round_about = goes_round(layer, side, piece)
+            if round_about is not None:
+                @pl.when(round_about)
+                def _():
+                    detour(layer, side, piece).start()
 
     def send(layer, pieces):
         @pl.when(has_up)
         def _():
-            send_side(layer, 0, pieces)
+            send_direct(layer, 0, pieces)
 
         @pl.when(has_down)
         def _():
-            send_side(layer, 1, pieces)
+            send_direct(layer, 1, pieces)
+
+        send_round(layer, 1, pieces)
+
+    def passed(layer, side, piece):
+        slot = RELAYED[layer].index(piece)
+        if side == 0:
+            return jnp.logical_and(passes_up, is_relayed(layer, slot, up_count(run_index + 1)))
+        return jnp.logical_and(passes_down, is_relayed(layer, slot, down_count(run_index - 1)))
+
+    def pass_on(layer, side, piece):
+        @pl.when(passed(layer, side, piece))
+        def _():
+            start, width = SENT[layer][piece]
+            part = relays[layer].at[:, start:start + width]
+            pltpu.make_async_remote_copy(
+                src_ref=part, dst_ref=part, send_sem=send_sem.at[0, 0], recv_sem=relay_sem.at[slot_of(layer, piece)],
+                device_id=above, device_id_type=MESH,
+            ).wait_recv()
+            onward(layer, side, piece).start()
+
+    def passed_on(layer, side, piece):
+        @pl.when(passed(layer, side, piece))
+        def _():
+            onward(layer, side, piece).wait_send()
 
     def awaited(layer, piece, rows):
         start, width = SENT[layer][piece]
@@ -122,30 +222,51 @@
         ).wait_send()
 
     all_first = range(len(SENT[0]))
-
-    @pl.when(jnp.logical_or(up_by_barrier, down_by_barrier))
-    def _():
-        pl.semaphore_wait(barrier, up_by_barrier.astype(jnp.int32) + down_by_barrier.astype(jnp.int32))
+    first_in_all = jnp.logical_and(opens, jnp.logical_not(later))
+
+    @pl.when(jnp.logical_not(first_in_all))
+    def _():
+        pl.semaphore_wait(
+            barrier,
+            up_by_barrier.astype(jnp.int32) + down_by_barrier.astype(jnp.int32) + closes.astype(jnp.int32)
+            + passes_down.astype(jnp.int32) + by_run_before.astype(jnp.int32),
+        )
+
+    @pl.when(down_by_barrier)
+    def _():
+        pl.semaphore_signal(ready_sem.at[1], inc=1, device_id=below, device_id_type=MESH)
+        send_direct(0, 1, all_first)
 
     @pl.when(up_by_barrier)
     def _():
         pl.semaphore_signal(ready_sem.at[0], inc=1, device_id=above, device_id_type=MESH)
-        send_side(0, 0, all_first)
-
-    @pl.when(down_by_barrier)
-    def _():
-        pl.semaphore_signal(ready_sem.at[1], inc=1, device_id=below, device_id_type=MESH)
-        send_side(0, 1, all_first)
+        send_direct(0, 0, all_first)
+
+    @pl.when(passes_down)
+    def _():
+        pl.semaphore_signal(ready_sem.at[2], inc=1, device_id=run_before, device_id_type=MESH)
+
+    @pl.when(by_run_after)
+    def _():
+        pl.semaphore_signal(ready_sem.at[3], inc=1, device_id=run_start, device_id_type=MESH)
+        pl.semaphore_wait(ready_sem.at[2], 1)
+
+    send_round(0, 1, all_first)
+    send_round(0, 0, all_first)
 
     @pl.when(down_by_ready)
     def _():
         pl.semaphore_wait(ready_sem.at[0], 1)
-        send_side(0, 1, all_first)
+        send_direct(0, 1, all_first)
 
     @pl.when(up_by_ready)
     def _():
         pl.semaphore_wait(ready_sem.at[1], 1)
-        send_side(0, 0, all_first)
+        send_direct(0, 0, all_first)
+
+    @pl.when(passes_up)
+    def _():
+        pl.semaphore_wait(ready_sem.at[3], 1)
 
     @pl.when(jnp.logical_not(has_up))
     def _():
@@ -215,6 +336,11 @@
             rest(layer, at, min(BLOCK, start + width - at), store)
 
     for piece in range(len(SENT[0])):
+        if piece < 3:
+            pass_on(0, 0, RELAYED[0][piece])
+            pass_on(0, 1, RELAYED[0][piece])
+        else:
+            pass_on(1, 1, RELAYED[1][piece - 3])
         arrived(0, piece)
         latmix(0, piece)
         run(0, *DONE[0][piece], keep)
@@ -230,6 +356,10 @@
         else:
             rest(1, *DONE[1][piece], finish)
 
+    for slot in range(3):
+        passed_on(0, 0, RELAYED[0][slot])
+        passed_on(0, 1, RELAYED[0][slot])
+        passed_on(1, 1, RELAYED[1][slot])
     for layer in range(LAYERS):
         @pl.when(has_up)
         def _():
@@ -257,11 +387,14 @@
             pltpu.VMEM((LAYERS, C), jnp.float32),
             pltpu.VMEM((LAYERS, C, H), jnp.bfloat16),
             pltpu.VMEM((LAYERS, H, C), jnp.bfloat16),
+            pltpu.VMEM((ROWS, LON, C), jnp.bfloat16),
+            pltpu.VMEM((ROWS, LON, C), jnp.bfloat16),
             pltpu.SemaphoreType.DMA((LAYERS, 2)),
             pltpu.SemaphoreType.DMA((len(SENT[0]),)),
             pltpu.SemaphoreType.DMA((len(SENT[1]),)),
             pltpu.SemaphoreType.DMA((6,)),
-            pltpu.SemaphoreType.REGULAR((2,)),
+            pltpu.SemaphoreType.REGULAR((4,)),
+            pltpu.SemaphoreType.DMA((6,)),
         ],
         compiler_params=pltpu.CompilerParams(collective_id=0, has_side_effects=True),
         name="step",

time: 35.1 us -> 33.6 us (0.957)
  the two profiles are of different devices: /device:TPU:6 before, /device:TPU:4 now
where the time goes in v3:
time: 33.6 us; the launch traced here: 33.5 us
  Pallas kernels  32.7 us (97%)
  local copies, waits for them, and re-layouts  0.82 us (2%)
    pallas_call x1, Pallas kernels, shards(): pl.pallas_call(kernel, out_shape=pltpu.VMEM(fields.shape, fields.dtype),...  32.7 us
    unnamed x1, local copies, waits for them, and re-layouts  0.82 us

profile of v3, /device:TPU:4, one launch (start us, length us, event | category | flops | bytes accessed | tf_op | source)
XLA Modules:
  0.0 33.5 jit_solution(18058166335570995715)
XLA Ops:
  0.0 32.7 %step.1 = bf16[1,4,576,128]{3,2,1,0:T(8,128)(2,1)S(1)} custom-call(bf16[1,4,576,128]{3,2,1,0:T(8,128)(2,1)} %fields.1, bf16[9,2,128]{2,1,0:T(2,128)(2,1)} %bitcast.2, bf16[9,2,128]{2,1,0:T(2,128)(2,1)} %bitcast.3, f32[2,128]{1,0:T(2,128)} %gains.1, bf16[2,128,256]{2,1,0:T(8,128)(2,1)} %w_in.1, bf16[2,256,128]{2,1,0:T(8,128)(2,1)} %w_out.1), custom_call_target="tpu_custom_call" | custom-call | tf_op jit(solution)/shard_map/step/pallas_call | solution.py:374
  32.7 0.8 %copy.8 = bf16[1,4,576,128]{3,2,1,0:T(8,128)(2,1)} copy(bf16[1,4,576,128]{3,2,1,0:T(8,128)(2,1)S(1)} %step.1) | data formatting | bytes 1179648

commit v4 on v2

--- a/solution.py
+++ b/solution.py
@@ -26,26 +26,35 @@
     ((16, 64), (80, 96), (176, 96), (272, 96), (368, 96), (464, 96)),
     ((32, 32), (64, 96), (160, 96), (256, 96), (352, 96), (448, 48), (496, 48), (544, 64)),
 )
+RELAYED = ((3, 4, 5), (0, 1, 2))
 NEXT = ((0,), (1,), (2,), (3,), (4,), (5, 6))
 
 
 def kernel(fields, lat_taps, lon_taps, gains, w_in, w_out, out,
            state0, state1, mixed, lat16, lon16, lat32, lon32, gain32, win, wout,
-           send_sem, recv0_sem, recv1_sem, load_sem, ready_sem):
+           relay0, relay1, send_sem, recv0_sem, recv1_sem, load_sem, ready_sem, relay_sem):
     band = lax.axis_index("band")
     place_in_run = lax.rem(band, RUN)
+    run_index = band // RUN
     opens = place_in_run == 0
     closes = place_in_run == RUN - 1
     has_up = band > 0
     has_down = band < BANDS - 1
     inside = jnp.logical_and(has_up, has_down)
-    up_by_barrier = jnp.logical_and(has_up, jnp.logical_not(opens))
-    up_by_ready = jnp.logical_and(has_up, opens)
-    down_by_barrier = jnp.logical_and(has_down, closes)
     down_by_ready = jnp.logical_and(has_down, jnp.logical_not(closes))
     states = (state0, state1)
     recv_sems = (recv0_sem, recv1_sem)
     above, below = {"band": band - 1}, {"band": band + 1}
+    run_before, run_after = {"band": band - RUN}, {"band": band + RUN}
+    run_start, run_end = {"band": band - (RUN - 1)}, {"band": band + (RUN - 1)}
+    relays = (relay0, relay1)
+    later, sooner = run_index > 0, run_index < BANDS // RUN - 1
+    sends_round = jnp.logical_and(closes, sooner)
+    passes = jnp.logical_and(closes, later)
+    greeted_late = jnp.logical_and(opens, later)
+
+    def is_relayed(layer, slot, count):
+        return count >= (len(RELAYED[0]) - slot if layer == 0 else slot + 1)
 
     barrier = pltpu.get_barrier_semaphore()
 
@@ -53,9 +62,15 @@
     def _():
         pl.semaphore_signal(barrier, inc=1, device_id=below, device_id_type=MESH)
 
-    @pl.when(up_by_ready)
+    @pl.when(sends_round)
+    def _():
+        pl.semaphore_signal(barrier, inc=1, device_id=below, device_id_type=MESH)
+        pl.semaphore_signal(barrier, inc=1, device_id=run_after, device_id_type=MESH)
+
+    @pl.when(greeted_late)
     def _():
         pl.semaphore_signal(barrier, inc=1, device_id=above, device_id_type=MESH)
+        pl.semaphore_signal(barrier, inc=1, device_id=run_end, device_id_type=MESH)
 
     own = pltpu.make_async_copy(fields.at[0], state0.at[ROWS:2 * ROWS, 0:LON], load_sem.at[0])
     loads = [
@@ -83,18 +98,84 @@
             device_id_type=MESH,
         )
 
-    def send_side(layer, side, pieces):
+    def slot_of(layer, piece):
+        return layer * len(RELAYED[0]) + RELAYED[layer].index(piece)
+
+    def detour(layer, piece):
+        start, width = SENT[layer][piece]
+        source = fields.at[0, :, start:start + width] if layer == 0 else state1.at[ROWS:2 * ROWS, start:start + width]
+        return pltpu.make_async_remote_copy(
+            src_ref=source,
+            dst_ref=relays[layer].at[:, start:start + width],
+            send_sem=send_sem.at[layer, 1],
+            recv_sem=relay_sem.at[slot_of(layer, piece)],
+            device_id=run_after,
+            device_id_type=MESH,
+        )
+
+    def onward(layer, piece):
+        start, width = SENT[layer][piece]
+        return pltpu.make_async_remote_copy(
+            src_ref=relays[layer].at[:, start:start + width],
+            dst_ref=states[layer].at[0:ROWS, start:start + width],
+            send_sem=relay_sem.at[slot_of(layer, piece)],
+            recv_sem=recv_sems[layer].at[piece],
+            device_id=run_start,
+            device_id_type=MESH,
+        )
+
+    def goes_round(layer, piece):
+        return jnp.logical_and(sends_round, is_relayed(layer, RELAYED[layer].index(piece), run_index + 1))
+
+    def send_up(layer, pieces):
         for piece in pieces:
-            copy(layer, side, piece).start()
+            copy(layer, 0, piece).start()
+
+    def send_down(layer, pieces):
+        for piece in pieces:
+            if piece not in RELAYED[layer]:
+                copy(layer, 1, piece).start()
+            else:
+                @pl.when(jnp.logical_not(goes_round(layer, piece)))
+                def _():
+                    copy(layer, 1, piece).start()
+
+    def send_round(layer, pieces):
+        for piece in pieces:
+            if piece in RELAYED[layer]:
+                @pl.when(goes_round(layer, piece))
+                def _():
+                    detour(layer, piece).start()
 
     def send(layer, pieces):
+        send_round(layer, pieces)
+
+        @pl.when(has_down)
+        def _():
+            send_down(layer, pieces)
+
         @pl.when(has_up)
         def _():
-            send_side(layer, 0, pieces)
-
-        @pl.when(has_down)
-        def _():
-            send_side(layer, 1, pieces)
+            send_up(layer, pieces)
+
+    def passed(layer, piece):
+        return jnp.logical_and(passes, is_relayed(layer, RELAYED[layer].index(piece), run_index))
+
+    def pass_on(layer, piece):
+        @pl.when(passed(layer, piece))
+        def _():
+            start, width = SENT[layer][piece]
+            part = relays[layer].at[:, start:start + width]
+            pltpu.make_async_remote_copy(
+                src_ref=part, dst_ref=part, send_sem=send_sem.at[0, 0], recv_sem=relay_sem.at[slot_of(layer, piece)],
+                device_id=above, device_id_type=MESH,
+            ).wait_recv()
+            onward(layer, piece).start()
+
+    def passed_on(layer, piece):
+        @pl.when(passed(layer, piece))
+        def _():
+            onward(layer, piece).wait_send()
 
     def awaited(layer, piece, rows):
         start, width = SENT[layer][piece]
@@ -123,29 +204,37 @@
 
     all_first = range(len(SENT[0]))
 
-    @pl.when(jnp.logical_or(up_by_barrier, down_by_barrier))
-    def _():
-        pl.semaphore_wait(barrier, up_by_barrier.astype(jnp.int32) + down_by_barrier.astype(jnp.int32))
-
-    @pl.when(up_by_barrier)
-    def _():
+    @pl.when(jnp.logical_not(opens))
+    def _():
+        pl.semaphore_wait(barrier, 1 + sends_round.astype(jnp.int32) + 2 * passes.astype(jnp.int32))
         pl.semaphore_signal(ready_sem.at[0], inc=1, device_id=above, device_id_type=MESH)
-        send_side(0, 0, all_first)
-
-    @pl.when(down_by_barrier)
-    def _():
-        pl.semaphore_signal(ready_sem.at[1], inc=1, device_id=below, device_id_type=MESH)
-        send_side(0, 1, all_first)
+
+    @pl.when(passes)
+    def _():
+        pl.semaphore_signal(ready_sem.at[1], inc=1, device_id=run_before, device_id_type=MESH)
+
+    @pl.when(sends_round)
+    def _():
+        send_down(0, all_first)
+
+    @pl.when(jnp.logical_not(opens))
+    def _():
+        send_up(0, all_first)
+
+    @pl.when(sends_round)
+    def _():
+        pl.semaphore_wait(ready_sem.at[1], 1)
+        send_round(0, all_first)
 
     @pl.when(down_by_ready)
     def _():
         pl.semaphore_wait(ready_sem.at[0], 1)
-        send_side(0, 1, all_first)
-
-    @pl.when(up_by_ready)
-    def _():
-        pl.semaphore_wait(ready_sem.at[1], 1)
-        send_side(0, 0, all_first)
+        send_down(0, all_first)
+
+    @pl.when(greeted_late)
+    def _():
+        pl.semaphore_wait(barrier, 1)
+        send_up(0, all_first)
 
     @pl.when(jnp.logical_not(has_up))
     def _():
@@ -215,6 +304,10 @@
             rest(layer, at, min(BLOCK, start + width - at), store)
 
     for piece in range(len(SENT[0])):
+        if piece < 3:
+            pass_on(0, RELAYED[0][piece])
+        else:
+            pass_on(1, RELAYED[1][piece - 3])
         arrived(0, piece)
         latmix(0, piece)
         run(0, *DONE[0][piece], keep)
@@ -230,6 +323,9 @@
         else:
             rest(1, *DONE[1][piece], finish)
 
+    for slot in range(3):
+        passed_on(0, RELAYED[0][slot])
+        passed_on(1, RELAYED[1][slot])
     for layer in range(LAYERS):
         @pl.when(has_up)
         def _():
@@ -257,11 +353,14 @@
             pltpu.VMEM((LAYERS, C), jnp.float32),
             pltpu.VMEM((LAYERS, C, H), jnp.bfloat16),
             pltpu.VMEM((LAYERS, H, C), jnp.bfloat16),
+            pltpu.VMEM((ROWS, LON, C), jnp.bfloat16),
+            pltpu.VMEM((ROWS, LON, C), jnp.bfloat16),
             pltpu.SemaphoreType.DMA((LAYERS, 2)),
             pltpu.SemaphoreType.DMA((len(SENT[0]),)),
             pltpu.SemaphoreType.DMA((len(SENT[1]),)),
             pltpu.SemaphoreType.DMA((6,)),
             pltpu.SemaphoreType.REGULAR((2,)),
+            pltpu.SemaphoreType.DMA((6,)),
         ],
         compiler_params=pltpu.CompilerParams(collective_id=0, has_side_effects=True),
         name="step",

time: 35.1 us -> 32.8 us (0.934)
  Pallas kernels: 34.2 us -> 31.8 us
    pallas_call x1, Pallas kernels: 34.2 us -> 31.8 us  [shards(): pl.pallas_call(kernel, out_shape=pltpu.VMEM(fields.shape, fields.dtype),...]
where the time goes in v4:
time: 32.8 us; the launch traced here: 32.7 us
  Pallas kernels  31.8 us (97%)
  local copies, waits for them, and re-layouts  0.82 us (2%)
    pallas_call x1, Pallas kernels, shards(): pl.pallas_call(kernel, out_shape=pltpu.VMEM(fields.shape, fields.dtype),...  31.8 us
    unnamed x1, local copies, waits for them, and re-layouts  0.82 us

profile of v4, /device:TPU:6, one launch (start us, length us, event | category | flops | bytes accessed | tf_op | source)
XLA Modules:
  0.0 32.7 jit_solution(1666839704638716839)
XLA Ops:
  0.0 31.8 %step.1 = bf16[1,4,576,128]{3,2,1,0:T(8,128)(2,1)S(1)} custom-call(bf16[1,4,576,128]{3,2,1,0:T(8,128)(2,1)} %fields.1, bf16[9,2,128]{2,1,0:T(2,128)(2,1)} %bitcast.2, bf16[9,2,128]{2,1,0:T(2,128)(2,1)} %bitcast.3, f32[2,128]{1,0:T(2,128)} %gains.1, bf16[2,128,256]{2,1,0:T(8,128)(2,1)} %w_in.1, bf16[2,256,128]{2,1,0:T(8,128)(2,1)} %w_out.1), custom_call_target="tpu_custom_call" | custom-call | tf_op jit(solution)/shard_map/step/pallas_call | solution.py:340
  31.9 0.8 %copy.8 = bf16[1,4,576,128]{3,2,1,0:T(8,128)(2,1)} copy(bf16[1,4,576,128]{3,2,1,0:T(8,128)(2,1)S(1)} %step.1) | data formatting | bytes 1179648

commit v5 on v3

--- a/solution.py
+++ b/solution.py
@@ -14,6 +14,7 @@
 H = 256
 BANDS = 32
 RUN = 8
+RUNS = BANDS // RUN
 PAD = 16
 BLOCK = 48
 MESH = pl.DeviceIdType.MESH
@@ -41,48 +42,34 @@
     has_up = band > 0
     has_down = band < BANDS - 1
     inside = jnp.logical_and(has_up, has_down)
-    up_by_barrier = jnp.logical_and(has_up, jnp.logical_not(opens))
-    up_by_ready = jnp.logical_and(has_up, opens)
-    down_by_barrier = jnp.logical_and(has_down, closes)
-    down_by_ready = jnp.logical_and(has_down, jnp.logical_not(closes))
+    tied_above = place_in_run >= RUN - 2
+    tied_below = jnp.logical_and(place_in_run >= RUN - 3, jnp.logical_not(closes))
     states = (state0, state1)
     recv_sems = (recv0_sem, recv1_sem)
     above, below = {"band": band - 1}, {"band": band + 1}
     run_before, run_after = {"band": band - RUN}, {"band": band + RUN}
     run_start, run_end = {"band": band - (RUN - 1)}, {"band": band + (RUN - 1)}
     relays = (relay0, relay1)
-    later, sooner = run_index > 0, run_index < BANDS // RUN - 1
-    by_run_after = jnp.logical_and(closes, sooner)
-    by_run_before = jnp.logical_and(opens, later)
+    later, sooner = run_index > 0, run_index < RUNS - 1
+    round_down = jnp.logical_and(closes, sooner)
+    round_up = jnp.logical_and(opens, later)
     passes_down = jnp.logical_and(closes, later)
     passes_up = jnp.logical_and(opens, sooner)
 
-    def down_count(run):
-        return run + 1
-
-    def up_count(run):
-        return BANDS // RUN - run
-
     def is_relayed(layer, slot, count):
         return count >= (len(RELAYED[0]) - slot if layer == 0 else slot + 1)
 
     barrier = pltpu.get_barrier_semaphore()
 
-    @pl.when(down_by_ready)
-    def _():
-        pl.semaphore_signal(barrier, inc=1, device_id=below, device_id_type=MESH)
-
-    @pl.when(up_by_ready)
-    def _():
-        pl.semaphore_signal(barrier, inc=1, device_id=above, device_id_type=MESH)
-
-    @pl.when(opens)
-    def _():
-        pl.semaphore_signal(barrier, inc=1, device_id=run_end, device_id_type=MESH)
-
-    @pl.when(jnp.logical_and(sooner, jnp.logical_or(opens, closes)))
-    def _():
-        pl.semaphore_signal(barrier, inc=1, device_id=run_after, device_id_type=MESH)
+    def greet(condition, device):
+        @pl.when(condition)
+        def _():
+            pl.semaphore_signal(barrier, inc=1, device_id=device, device_id_type=MESH)
+
+    greet(jnp.logical_or(place_in_run < RUN - 2, round_down), below)
+    greet(jnp.logical_or(tied_above, round_up), above)
+    greet(opens, run_end)
+    greet(jnp.logical_or(round_down, passes_up), run_after)
 
     own = pltpu.make_async_copy(fields.at[0], state0.at[ROWS:2 * ROWS, 0:LON], load_sem.at[0])
     loads = [
@@ -142,8 +129,8 @@
             return None
         slot = RELAYED[layer].index(piece)
         if side == 0:
-            return jnp.logical_and(by_run_before, is_relayed(layer, slot, up_count(run_index)))
-        return jnp.logical_and(by_run_after, is_relayed(layer, slot, down_count(run_index)))
+            return jnp.logical_and(round_up, is_relayed(layer, slot, RUNS - run_index))
+        return jnp.logical_and(round_down, is_relayed(layer, slot, run_index + 1))
 
     def send_direct(layer, side, pieces):
         for piece in pieces:
@@ -155,6 +142,12 @@
                 def _():
                     copy(layer, side, piece).start()
 
+    def send_up(layer, pieces):
+        send_direct(layer, 0, pieces)
+
+    def send_down(layer, pieces):
+        send_direct(layer, 1, pieces)
+
     def send_round(layer, side, pieces):
         for piece in pieces:
             round_about = goes_round(layer, side, piece)
@@ -164,21 +157,21 @@
                     detour(layer, side, piece).start()
 
     def send(layer, pieces):
+        send_round(layer, 1, pieces)
+
+        @pl.when(has_down)
+        def _():
+            send_down(layer, pieces)
+
         @pl.when(has_up)
         def _():
-            send_direct(layer, 0, pieces)
-
-        @pl.when(has_down)
-        def _():
-            send_direct(layer, 1, pieces)
-
-        send_round(layer, 1, pieces)
+            send_up(layer, pieces)
 
     def passed(layer, side, piece):
         slot = RELAYED[layer].index(piece)
         if side == 0:
-            return jnp.logical_and(passes_up, is_relayed(layer, slot, up_count(run_index + 1)))
-        return jnp.logical_and(passes_down, is_relayed(layer, slot, down_count(run_index - 1)))
+            return jnp.logical_and(passes_up, is_relayed(layer, slot, RUNS - 1 - run_index))
+        return jnp.logical_and(passes_down, is_relayed(layer, slot, run_index))
 
     def pass_on(layer, side, piece):
         @pl.when(passed(layer, side, piece))
@@ -222,51 +215,55 @@
         ).wait_send()
 
     all_first = range(len(SENT[0]))
-    first_in_all = jnp.logical_and(opens, jnp.logical_not(later))
-
-    @pl.when(jnp.logical_not(first_in_all))
-    def _():
-        pl.semaphore_wait(
-            barrier,
-            up_by_barrier.astype(jnp.int32) + down_by_barrier.astype(jnp.int32) + closes.astype(jnp.int32)
-            + passes_down.astype(jnp.int32) + by_run_before.astype(jnp.int32),
-        )
-
-    @pl.when(down_by_barrier)
-    def _():
-        pl.semaphore_signal(ready_sem.at[1], inc=1, device_id=below, device_id_type=MESH)
-        send_direct(0, 1, all_first)
-
-    @pl.when(up_by_barrier)
-    def _():
-        pl.semaphore_signal(ready_sem.at[0], inc=1, device_id=above, device_id_type=MESH)
-        send_direct(0, 0, all_first)
-
-    @pl.when(passes_down)
-    def _():
-        pl.semaphore_signal(ready_sem.at[2], inc=1, device_id=run_before, device_id_type=MESH)
-
-    @pl.when(by_run_after)
-    def _():
-        pl.semaphore_signal(ready_sem.at[3], inc=1, device_id=run_start, device_id_type=MESH)
-        pl.semaphore_wait(ready_sem.at[2], 1)
-
-    send_round(0, 1, all_first)
-    send_round(0, 0, all_first)
-
-    @pl.when(down_by_ready)
+
+    def answer(condition, which, device):
+        @pl.when(condition)
+        def _():
+            pl.semaphore_signal(ready_sem.at[which], inc=1, device_id=device, device_id_type=MESH)
+
+    @pl.when(jnp.logical_not(opens))
+    def _():
+        pl.semaphore_wait(barrier, 1 + (tied_below | round_down).astype(jnp.int32) + passes_down.astype(jnp.int32))
+
+    @pl.when(tied_below | round_down)
+    def _():
+        send_down(0, all_first)
+
+    answer(passes_down, 1, run_before)
+    answer(round_down, 1, run_start)
+    answer(jnp.logical_and(place_in_run > 0, place_in_run < RUN - 2), 0, above)
+    answer(place_in_run == RUN - 2, 0, below)
+
+    @pl.when(jnp.logical_not(opens | closes))
+    def _():
+        send_up(0, all_first)
+
+    @pl.when(round_down)
+    def _():
+        pl.semaphore_wait(ready_sem.at[1], 1)
+        send_round(0, 1, all_first)
+
+    @pl.when(jnp.logical_not(tied_below))
     def _():
         pl.semaphore_wait(ready_sem.at[0], 1)
-        send_direct(0, 1, all_first)
-
-    @pl.when(up_by_ready)
+
+        @pl.when(closes)
+        def _():
+            send_up(0, all_first)
+
+        @pl.when(jnp.logical_not(closes))
+        def _():
+            send_down(0, all_first)
+
+    @pl.when(round_up)
+    def _():
+        pl.semaphore_wait(barrier, 2)
+        send_up(0, all_first)
+        send_round(0, 0, all_first)
+
+    @pl.when(passes_up)
     def _():
         pl.semaphore_wait(ready_sem.at[1], 1)
-        send_direct(0, 0, all_first)
-
-    @pl.when(passes_up)
-    def _():
-        pl.semaphore_wait(ready_sem.at[3], 1)
 
     @pl.when(jnp.logical_not(has_up))
     def _():
@@ -337,13 +334,13 @@
 
     for piece in range(len(SENT[0])):
         if piece < 3:
+            pass_on(0, 1, RELAYED[0][piece])
             pass_on(0, 0, RELAYED[0][piece])
-            pass_on(0, 1, RELAYED[0][piece])
-        else:
-            pass_on(1, 1, RELAYED[1][piece - 3])
         arrived(0, piece)
         latmix(0, piece)
         run(0, *DONE[0][piece], keep)
+        if piece in (2, 3, 4):
+            pass_on(1, 1, RELAYED[1][piece - 2])
         send(1, NEXT[piece])
     run(0, LON - 16, 32, keep)
     send(1, (len(SENT[1]) - 1,))
@@ -393,7 +390,7 @@
             pltpu.SemaphoreType.DMA((len(SENT[0]),)),
             pltpu.SemaphoreType.DMA((len(SENT[1]),)),
             pltpu.SemaphoreType.DMA((6,)),
-            pltpu.SemaphoreType.REGULAR((4,)),
+            pltpu.SemaphoreType.REGULAR((2,)),
             pltpu.SemaphoreType.DMA((6,)),
         ],
         compiler_params=pltpu.CompilerParams(collective_id=0, has_side_effects=True),

time: 33.6 us -> 32 us (0.952)
  the two profiles are of different devices: /device:TPU:4 before, /device:TPU:6 now
where the time goes in v5:
time: 32 us; the launch traced here: 31.9 us
  Pallas kernels  31.1 us (97%)
  local copies, waits for them, and re-layouts  0.82 us (3%)
    pallas_call x1, Pallas kernels, shards(): pl.pallas_call(kernel, out_shape=pltpu.VMEM(fields.shape, fields.dtype),...  31.1 us
    unnamed x1, local copies, waits for them, and re-layouts  0.82 us

profile of v5, /device:TPU:6, one launch (start us, length us, event | category | flops | bytes accessed | tf_op | source)
XLA Modules:
  0.0 31.9 jit_solution(10821786289832663271)
XLA Ops:
  0.0 31.1 %step.1 = bf16[1,4,576,128]{3,2,1,0:T(8,128)(2,1)S(1)} custom-call(bf16[1,4,576,128]{3,2,1,0:T(8,128)(2,1)} %fields.1, bf16[9,2,128]{2,1,0:T(2,128)(2,1)} %bitcast.2, bf16[9,2,128]{2,1,0:T(2,128)(2,1)} %bitcast.3, f32[2,128]{1,0:T(2,128)} %gains.1, bf16[2,128,256]{2,1,0:T(8,128)(2,1)} %w_in.1, bf16[2,256,128]{2,1,0:T(8,128)(2,1)} %w_out.1), custom_call_target="tpu_custom_call" | custom-call | tf_op jit(solution)/shard_map/step/pallas_call | solution.py:371
  31.1 0.8 %copy.8 = bf16[1,4,576,128]{3,2,1,0:T(8,128)(2,1)} copy(bf16[1,4,576,128]{3,2,1,0:T(8,128)(2,1)S(1)} %step.1) | data formatting | bytes 1179648

commit v6 on v5

--- a/solution.py
+++ b/solution.py
@@ -21,14 +21,14 @@
 
 SENT = (
     ((0, 96), (96, 96), (192, 96), (288, 96), (384, 96), (480, 96)),
-    ((16, 64), (80, 96), (176, 96), (272, 96), (368, 96), (464, 48), (512, 48), (560, 32)),
+    ((16, 64), (80, 96), (176, 96), (272, 96), (368, 96), (464, 64), (528, 64)),
 )
 DONE = (
     ((16, 64), (80, 96), (176, 96), (272, 96), (368, 96), (464, 96)),
-    ((32, 32), (64, 96), (160, 96), (256, 96), (352, 96), (448, 48), (496, 48), (544, 64)),
+    ((32, 32), (64, 96), (160, 96), (256, 96), (352, 96), (448, 64), (512, 96)),
 )
 RELAYED = ((3, 4, 5), (0, 1, 2))
-NEXT = ((0,), (1,), (2,), (3,), (4,), (5, 6))
+NEXT = ((0,), (1,), (2,), (3,), (4,), (5,))
 
 
 def kernel(fields, lat_taps, lon_taps, gains, w_in, w_out, out,
@@ -348,10 +348,7 @@
     for piece in range(len(SENT[1])):
         arrived(1, piece)
         latmix(1, piece)
-        if piece < len(SENT[1]) - 1:
-            run(1, *DONE[1][piece], finish)
-        else:
-            rest(1, *DONE[1][piece], finish)
+        run(1, *DONE[1][piece], finish)
 
     for slot in range(3):
         passed_on(0, 0, RELAYED[0][slot])

time: 32 us -> 31.6 us (0.988)
  Pallas kernels: 31.1 us -> 30.7 us
    pallas_call x1, Pallas kernels: 31.1 us -> 30.7 us  [shards(): pl.pallas_call(kernel, out_shape=pltpu.VMEM(fields.shape, fields.dtype),...]
where the time goes in v6:
time: 31.6 us; the launch traced here: 31.5 us
  Pallas kernels  30.7 us (97%)
  local copies, waits for them, and re-layouts  0.82 us (3%)
    pallas_call x1, Pallas kernels, shards(): pl.pallas_call(kernel, out_shape=pltpu.VMEM(fields.shape, fields.dtype),...  30.7 us
    unnamed x1, local copies, waits for them, and re-layouts  0.82 us

profile of v6, /device:TPU:6, one launch (start us, length us, event | category | flops | bytes accessed | tf_op | source)
XLA Modules:
  0.0 31.5 jit_solution(15369938632512313683)
XLA Ops:
  0.0 30.7 %step.1 = bf16[1,4,576,128]{3,2,1,0:T(8,128)(2,1)S(1)} custom-call(bf16[1,4,576,128]{3,2,1,0:T(8,128)(2,1)} %fields.1, bf16[9,2,128]{2,1,0:T(2,128)(2,1)} %bitcast.2, bf16[9,2,128]{2,1,0:T(2,128)(2,1)} %bitcast.3, f32[2,128]{1,0:T(2,128)} %gains.1, bf16[2,128,256]{2,1,0:T(8,128)(2,1)} %w_in.1, bf16[2,256,128]{2,1,0:T(8,128)(2,1)} %w_out.1), custom_call_target="tpu_custom_call" | custom-call | tf_op jit(solution)/shard_map/step/pallas_call | solution.py:368
  30.7 0.8 %copy.8 = bf16[1,4,576,128]{3,2,1,0:T(8,128)(2,1)} copy(bf16[1,4,576,128]{3,2,1,0:T(8,128)(2,1)S(1)} %step.1) | data formatting | bytes 1179648

commit v7 on v6

--- a/solution.py
+++ b/solution.py
@@ -17,6 +17,8 @@
 RUNS = BANDS // RUN
 PAD = 16
 BLOCK = 48
+TAIL = 512
+TAIL_WIDTH = 96
 MESH = pl.DeviceIdType.MESH
 
 SENT = (
@@ -25,14 +27,60 @@
 )
 DONE = (
     ((16, 64), (80, 96), (176, 96), (272, 96), (368, 96), (464, 96)),
-    ((32, 32), (64, 96), (160, 96), (256, 96), (352, 96), (448, 64), (512, 96)),
+    ((32, 32), (64, 96), (160, 96), (256, 96), (352, 96), (448, 64)),
 )
 RELAYED = ((3, 4, 5), (0, 1, 2))
 NEXT = ((0,), (1,), (2,), (3,), (4,), (5,))
 
 
-def kernel(fields, lat_taps, lon_taps, gains, w_in, w_out, out,
-           state0, state1, mixed, lat16, lon16, lat32, lon32, gain32, win, wout,
+def pointwise(mixes, lon_tap, gain, proj_in, proj_out):
+    totals = []
+    for mix in mixes:
+        total = mix(0) * lon_tap(0)
+        for k in range(1, TAPS):
+            total = total + mix(3 * k) * lon_tap(k)
+        totals.append(total)
+    total = jnp.concatenate(totals, axis=0)
+    mean = jnp.mean(total, axis=-1, keepdims=True)
+    centred = total - mean
+    var = jnp.mean(centred * centred, axis=-1, keepdims=True)
+    normed = (centred * lax.rsqrt(var + 1e-06) * gain).astype(jnp.bfloat16)
+    inner = jnp.dot(normed, proj_in, preferred_element_type=jnp.float32)
+    hidden = (0.5 * inner * (1.0 + lax.erf(inner * 0.7071067811865476))).astype(jnp.bfloat16)
+    return jnp.dot(hidden, proj_out, preferred_element_type=jnp.float32)
+
+
+def finishing(done, mix, old, lon32, gain32, win, wout, out, last, sems):
+    layer = LAYERS - 1
+    copies = [pltpu.make_async_copy(done, out.at[0, :, 32:TAIL], sems.at[0])]
+    copies[0].start()
+    for block in range(TAIL_WIDTH // BLOCK):
+        at = block * BLOCK
+
+        def shifted(i):
+            return lambda by: mix[i, 16 + at - REACH + by:16 + at - REACH + by + BLOCK, :]
+
+        delta = pointwise(
+            [shifted(i) for i in range(ROWS)], lambda k: lon32[k, layer:layer + 1, :], gain32[layer:layer + 1, :],
+            win[layer], wout[layer],
+        )
+        for i in range(ROWS):
+            value = old[i, at:at + BLOCK, :].astype(jnp.float32) + delta[i * BLOCK:(i + 1) * BLOCK]
+            last[i, at:at + BLOCK, :] = value.astype(jnp.bfloat16)
+        if block == 0:
+            copies.append(pltpu.make_async_copy(last.at[:, 0:BLOCK], out.at[0, :, TAIL:TAIL + BLOCK], sems.at[1]))
+            copies[-1].start()
+    inside = LON - TAIL
+    copies.append(pltpu.make_async_copy(last.at[:, BLOCK:inside], out.at[0, :, TAIL + BLOCK:LON], sems.at[2]))
+    copies.append(pltpu.make_async_copy(last.at[:, inside:], out.at[0, :, 0:TAIL_WIDTH - inside], sems.at[3]))
+    copies[-2].start()
+    copies[-1].start()
+    for started in copies:
+        started.wait()
+
+
+def kernel(fields, lat_taps, lon_taps, gains, w_in, w_out, done, mix, old, lon32, gain32, win, wout,
+           state0, state1, mixed, lat16, lon16, lat32,
            relay0, relay1, send_sem, recv0_sem, recv1_sem, load_sem, ready_sem, relay_sem):
     band = lax.axis_index("band")
     place_in_run = lax.rem(band, RUN)
@@ -292,29 +340,28 @@
                 for k in range(1, TAPS):
                     total = total + rows[i + k] * lat32[k, layer:layer + 1, :]
                 total = total.astype(jnp.bfloat16).astype(jnp.float32)
-                mixed[layer, i, PAD + at:PAD + at + 16, :] = total
+                if layer == 0 or at <= TAIL:
+                    mixed[layer, i, PAD + at:PAD + at + 16, :] = total
+                if layer == 1 and at >= TAIL - 16:
+                    mix[i, at - TAIL + 16:at - TAIL + 32, :] = total
                 if at + LON < (LAYERS + 1) * 16 + LON + layer * 16 - 16:
-                    mixed[layer, i, PAD + at + LON:PAD + at + LON + 16, :] = total
+                    if layer == 0:
+                        mixed[layer, i, PAD + at + LON:PAD + at + LON + 16, :] = total
+                    else:
+                        mix[i, at + LON - TAIL + 16:at + LON - TAIL + 32, :] = total
 
     def rest(layer, start, width, store):
-        totals = []
+        def shifted(i):
+            at = PAD + start - REACH
+            return lambda by: mixed[layer, i, at + by:at + by + width, :]
+
+        delta = pointwise(
+            [shifted(i) for i in range(ROWS)], lambda k: lon32[k, layer:layer + 1, :], gain32[layer:layer + 1, :],
+            win[layer], wout[layer],
+        )
         for i in range(ROWS):
-            at = PAD + start - REACH
-            total = mixed[layer, i, at:at + width, :] * lon32[0, layer:layer + 1, :]
-            for k in range(1, TAPS):
-                total = total + mixed[layer, i, at + 3 * k:at + 3 * k + width, :] * lon32[k, layer:layer + 1, :]
-            totals.append(total)
-        total = jnp.concatenate(totals, axis=0)
-        mean = jnp.mean(total, axis=-1, keepdims=True)
-        centred = total - mean
-        var = jnp.mean(centred * centred, axis=-1, keepdims=True)
-        normed = (centred * lax.rsqrt(var + 1e-06) * gain32[layer:layer + 1, :]).astype(jnp.bfloat16)
-        inner = jnp.dot(normed, win[layer], preferred_element_type=jnp.float32)
-        hidden = (0.5 * inner * (1.0 + lax.erf(inner * 0.7071067811865476))).astype(jnp.bfloat16)
-        delta = jnp.dot(hidden, wout[layer], preferred_element_type=jnp.float32)
-        for i in range(ROWS):
-            old = states[layer][ROWS + i, start:start + width, :].astype(jnp.float32)
-            store(i, start, width, (old + delta[i * width:(i + 1) * width]).astype(jnp.bfloat16))
+            before = states[layer][ROWS + i, start:start + width, :].astype(jnp.float32)
+            store(i, start, width, (before + delta[i * width:(i + 1) * width]).astype(jnp.bfloat16))
 
     def keep(i, start, width, value):
         state1[ROWS + i, start:start + width, :] = value
@@ -322,11 +369,7 @@
             state1[ROWS + i, LON + 16:LON + 32, :] = value[:16]
 
     def finish(i, start, width, value):
-        if start + width <= LON:
-            out[0, i, start:start + width, :] = value
-        else:
-            out[0, i, start:LON, :] = value[:LON - start]
-            out[0, i, 0:start + width - LON, :] = value[LON - start:]
+        done[i, start - 32:start - 32 + width, :] = value
 
     def run(layer, start, width, store):
         for at in range(start, start + width, BLOCK):
@@ -345,10 +388,12 @@
     run(0, LON - 16, 32, keep)
     send(1, (len(SENT[1]) - 1,))
 
+    old[...] = state1[ROWS:2 * ROWS, TAIL:TAIL + TAIL_WIDTH, :]
     for piece in range(len(SENT[1])):
         arrived(1, piece)
         latmix(1, piece)
-        run(1, *DONE[1][piece], finish)
+        if piece < len(DONE[1]):
+            run(1, *DONE[1][piece], finish)
 
     for slot in range(3):
         passed_on(0, 0, RELAYED[0][slot])
@@ -365,11 +410,20 @@
 
 
 def shards(fields, lat_taps, lon_taps, gains, w_in, w_out):
-    return pl.pallas_call(
+    kept = (
+        pltpu.VMEM((ROWS, TAIL - 32, C), jnp.bfloat16),
+        pltpu.VMEM((ROWS, TAIL_WIDTH + 32, C), jnp.float32),
+        pltpu.VMEM((ROWS, TAIL_WIDTH, C), jnp.bfloat16),
+        pltpu.VMEM((TAPS, LAYERS, C), jnp.float32),
+        pltpu.VMEM((LAYERS, C), jnp.float32),
+        pltpu.VMEM((LAYERS, C, H), jnp.bfloat16),
+        pltpu.VMEM((LAYERS, H, C), jnp.bfloat16),
+    )
+    handed = pl.pallas_call(
         kernel,
-        out_shape=pltpu.VMEM(fields.shape, fields.dtype),
+        out_shape=kept,
         in_specs=[pl.BlockSpec(memory_space=pl.ANY)] * 6,
-        out_specs=pl.BlockSpec(memory_space=pltpu.VMEM),
+        out_specs=[pl.BlockSpec(memory_space=pltpu.VMEM)] * len(kept),
         scratch_shapes=[
             pltpu.VMEM((3 * ROWS, LON + 32, C), jnp.bfloat16),
             pltpu.VMEM((3 * ROWS, LON + 32, C), jnp.bfloat16),
@@ -377,10 +431,6 @@
             pltpu.VMEM((TAPS, LAYERS, C), jnp.bfloat16),
             pltpu.VMEM((TAPS, LAYERS, C), jnp.bfloat16),
             pltpu.VMEM((TAPS, LAYERS, C), jnp.float32),
-            pltpu.VMEM((TAPS, LAYERS, C), jnp.float32),
-            pltpu.VMEM((LAYERS, C), jnp.float32),
-            pltpu.VMEM((LAYERS, C, H), jnp.bfloat16),
-            pltpu.VMEM((LAYERS, H, C), jnp.bfloat16),
             pltpu.VMEM((ROWS, LON, C), jnp.bfloat16),
             pltpu.VMEM((ROWS, LON, C), jnp.bfloat16),
             pltpu.SemaphoreType.DMA((LAYERS, 2)),
@@ -393,6 +443,16 @@
         compiler_params=pltpu.CompilerParams(collective_id=0, has_side_effects=True),
         name="step",
     )(fields, jnp.transpose(lat_taps, (1, 0, 2)), jnp.transpose(lon_taps, (1, 0, 2)), gains, w_in, w_out)
+    handed = [pltpu.with_memory_space_constraint(array, pltpu.VMEM) for array in handed]
+    return pl.pallas_call(
+        finishing,
+        out_shape=jax.ShapeDtypeStruct(fields.shape, fields.dtype),
+        in_specs=[pl.BlockSpec(memory_space=pltpu.VMEM)] * len(kept),
+        out_specs=pl.BlockSpec(memory_space=pl.ANY),
+        scratch_shapes=[pltpu.VMEM((ROWS, TAIL_WIDTH, C), jnp.bfloat16), pltpu.SemaphoreType.DMA((4,))],
+        compiler_params=pltpu.CompilerParams(vmem_limit_bytes=16 * 1024 * 1024),
+        name="finishing",
+    )(*handed)
 
 
 def solution(mesh):

time: 31.6 us -> 31.4 us (level)
  local copies, waits for them, and re-layouts: 0.82 us -> 0 us
  Pallas kernels: 30.7 us -> 31.3 us
    unnamed x1 -> x0, local copies, waits for them, and re-layouts: 0.82 us -> none
    pallas_call x1 -> x2, Pallas kernels: 30.7 us -> 31.3 us  [the longest x1 30.1 us: shards(): pl.pallas_call(kernel, out_shape=kept, in_specs=[pl.BlockSpec(memory_spac...]
where the time goes in v7:
time: 31.4 us
  Pallas kernels  31.3 us (100%)
    pallas_call x1, Pallas kernels, shards(): pl.pallas_call(kernel, out_shape=kept, in_specs=[pl.BlockSpec(memory_spac...  30.1 us
    pallas_call x1, Pallas kernels, shards(): pl.pallas_call(finishing, out_shape=jax.ShapeDtypeStruct(fields.shape, fi...  1.26 us

profile of v7, /device:TPU:6, one launch (start us, length us, event | category | flops | bytes accessed | tf_op | source)
XLA Modules:
  0.0 31.4 jit_solution(6676976479648144146)
XLA Ops:
  0.0 30.1 %step.1 = (bf16[4,480,128]{2,1,0:T(8,128)(2,1)S(1)}, f32[4,128,128]{2,1,0:T(8,128)S(1)}, bf16[4,96,128]{2,1,0:T(8,128)(2,1)S(1)}, f32[9,2,128]{2,1,0:T(2,128)S(1...) custom-call(bf16[1,4,576,128]{3,2,1,0:T(8,128)(2,1)} %fields.1, ...), custom_call_target="tpu_custom_call" | custom-call | tf_op jit(solution)/shard_map/step/pallas_call | solution.py:422
  30.1 1.3 %finishing.1 = bf16[1,4,576,128]{3,2,1,0:T(8,128)(2,1)} custom-call(bf16[4,480,128]{2,1,0:T(8,128)(2,1)S(1)} %get-tuple-element.12.done, f32[4,128,128]{2,1,0:T(8,128)S(1)} %get-tuple-element.13.mix, bf16[4,96,128]{2,1,0:T(8,128)(2,1)S(1)} %get-tuple-element.14.old, f32[9,2,128]{2,1,0:T(2,128)S(1)} %get-tuple-element.15.lon32, ...), custom_call_target="tpu_custom_call" | custom-call | tf_op jit(solution)/shard_map/finishing/pallas_call | solution.py:447

commit v8 on v7

--- a/solution.py
+++ b/solution.py
@@ -221,8 +221,14 @@
             return jnp.logical_and(passes_up, is_relayed(layer, slot, RUNS - 1 - run_index))
         return jnp.logical_and(passes_down, is_relayed(layer, slot, run_index))
 
-    def pass_on(layer, side, piece):
-        @pl.when(passed(layer, side, piece))
+    def pass_on(layer, side, piece, counts=(1, 2, 3)):
+        count = RUNS - 1 - run_index if side == 0 else run_index
+        now = passed(layer, side, piece)
+        for other in (1, 2, 3):
+            if other not in counts:
+                now = jnp.logical_and(now, count != other)
+
+        @pl.when(now)
         def _():
             start, width = SENT[layer][piece]
             part = relays[layer].at[:, start:start + width]
@@ -376,9 +382,10 @@
             rest(layer, at, min(BLOCK, start + width - at), store)
 
     for piece in range(len(SENT[0])):
-        if piece < 3:
-            pass_on(0, 1, RELAYED[0][piece])
-            pass_on(0, 0, RELAYED[0][piece])
+        for relayed, counts in (((3, (3,)), (4, (2,)), (5, (1,))), ((4, (3,)), (5, (2,))), ((5, (3,)),))[piece] if piece < 3 else ():
+            pass_on(0, 1, relayed, counts)
+        for relayed, counts in (((3, (3,)),), ((4, (2, 3)), (5, (1,))), ((5, (2, 3)),))[piece] if piece < 3 else ():
+            pass_on(0, 0, relayed, counts)
         arrived(0, piece)
         latmix(0, piece)
         run(0, *DONE[0][piece], keep)

time: 31.4 us -> 31.4 us (level)
  no operation moved by 1% of the time
where the time goes in v8:
time: 31.4 us
  Pallas kernels  31.3 us (100%)
    pallas_call x1, Pallas kernels, shards(): pl.pallas_call(kernel, out_shape=kept, in_specs=[pl.BlockSpec(memory_spac...  30.1 us
    pallas_call x1, Pallas kernels, shards(): pl.pallas_call(finishing, out_shape=jax.ShapeDtypeStruct(fields.shape, fi...  1.26 us

profile of v8, /device:TPU:6, one launch (start us, length us, event | category | flops | bytes accessed | tf_op | source)
XLA Modules:
  0.0 31.4 jit_solution(5739163944547410949)
XLA Ops:
  0.0 30.1 %step.1 = (bf16[4,480,128]{2,1,0:T(8,128)(2,1)S(1)}, f32[4,128,128]{2,1,0:T(8,128)S(1)}, bf16[4,96,128]{2,1,0:T(8,128)(2,1)S(1)}, f32[9,2,128]{2,1,0:T(2,128)S(1...) custom-call(bf16[1,4,576,128]{3,2,1,0:T(8,128)(2,1)} %fields.1, ...), custom_call_target="tpu_custom_call" | custom-call | tf_op jit(solution)/shard_map/step/pallas_call | solution.py:429
  30.1 1.3 %finishing.1 = bf16[1,4,576,128]{3,2,1,0:T(8,128)(2,1)} custom-call(bf16[4,480,128]{2,1,0:T(8,128)(2,1)S(1)} %get-tuple-element.12.done, f32[4,128,128]{2,1,0:T(8,128)S(1)} %get-tuple-element.13.mix, bf16[4,96,128]{2,1,0:T(8,128)(2,1)S(1)} %get-tuple-element.14.old, f32[9,2,128]{2,1,0:T(2,128)S(1)} %get-tuple-element.15.lon32, ...), custom_call_target="tpu_custom_call" | custom-call | tf_op jit(solution)/shard_map/finishing/pallas_call | solution.py:454

commit v9 on v8

--- a/solution.py
+++ b/solution.py
@@ -80,7 +80,7 @@
 
 
 def kernel(fields, lat_taps, lon_taps, gains, w_in, w_out, done, mix, old, lon32, gain32, win, wout,
-           state0, state1, mixed, lat16, lon16, lat32,
+           state0, state1, mixed, taps16, lat32,
            relay0, relay1, send_sem, recv0_sem, recv1_sem, load_sem, ready_sem, relay_sem):
     band = lax.axis_index("band")
     place_in_run = lax.rem(band, RUN)
@@ -121,11 +121,11 @@
 
     own = pltpu.make_async_copy(fields.at[0], state0.at[ROWS:2 * ROWS, 0:LON], load_sem.at[0])
     loads = [
-        pltpu.make_async_copy(lat_taps, lat16, load_sem.at[1]),
-        pltpu.make_async_copy(lon_taps, lon16, load_sem.at[2]),
-        pltpu.make_async_copy(gains, gain32, load_sem.at[3]),
-        pltpu.make_async_copy(w_in, win, load_sem.at[4]),
-        pltpu.make_async_copy(w_out, wout, load_sem.at[5]),
+        pltpu.make_async_copy(lat_taps, taps16.at[0], load_sem.at[1]),
+        pltpu.make_async_copy(lon_taps, taps16.at[1], load_sem.at[1]),
+        pltpu.make_async_copy(gains, gain32, load_sem.at[2]),
+        pltpu.make_async_copy(w_in, win, load_sem.at[3]),
+        pltpu.make_async_copy(w_out, wout, load_sem.at[4]),
     ]
     own.start()
     for load in loads:
@@ -330,11 +330,12 @@
             place[2 * ROWS:] = jnp.zeros((ROWS,) + place.shape[1:], place.dtype)
 
     own.wait()
-    for load in loads:
+    pltpu.make_async_copy(taps16, taps16, load_sem.at[1]).wait()
+    for load in loads[2:]:
         load.wait()
     state0[ROWS:2 * ROWS, LON:LON + 16, :] = state0[ROWS:2 * ROWS, 0:16, :]
-    lat32[...] = lat16[...].astype(jnp.float32)
-    lon32[...] = lon16[...].astype(jnp.float32)
+    lat32[...] = taps16[0].astype(jnp.float32)
+    lon32[...] = taps16[1].astype(jnp.float32)
 
     def latmix(layer, piece):
         place = states[layer]
@@ -435,15 +436,14 @@
             pltpu.VMEM((3 * ROWS, LON + 32, C), jnp.bfloat16),
             pltpu.VMEM((3 * ROWS, LON + 32, C), jnp.bfloat16),
             pltpu.VMEM((LAYERS, ROWS, PAD + LON + 64, C), jnp.float32),
-            pltpu.VMEM((TAPS, LAYERS, C), jnp.bfloat16),
-            pltpu.VMEM((TAPS, LAYERS, C), jnp.bfloat16),
+            pltpu.VMEM((2, TAPS, LAYERS, C), jnp.bfloat16),
             pltpu.VMEM((TAPS, LAYERS, C), jnp.float32),
             pltpu.VMEM((ROWS, LON, C), jnp.bfloat16),
             pltpu.VMEM((ROWS, LON, C), jnp.bfloat16),
             pltpu.SemaphoreType.DMA((LAYERS, 2)),
             pltpu.SemaphoreType.DMA((len(SENT[0]),)),
             pltpu.SemaphoreType.DMA((len(SENT[1]),)),
-            pltpu.SemaphoreType.DMA((6,)),
+            pltpu.SemaphoreType.DMA((5,)),
             pltpu.SemaphoreType.REGULAR((2,)),
             pltpu.SemaphoreType.DMA((6,)),
         ],

time: 31.4 us -> 31.4 us (level)
  no operation moved by 1% of the time
where the time goes in v9:
time: 31.4 us; the launch traced here: 31.3 us
  Pallas kernels  31.3 us (100%)
    pallas_call x1, Pallas kernels, shards(): pl.pallas_call(kernel, out_shape=kept, in_specs=[pl.BlockSpec(memory_spac...  30.1 us
    pallas_call x1, Pallas kernels, shards(): pl.pallas_call(finishing, out_shape=jax.ShapeDtypeStruct(fields.shape, fi...  1.26 us

profile of v9, /device:TPU:6, one launch (start us, length us, event | category | flops | bytes accessed | tf_op | source)
XLA Modules:
  0.0 31.3 jit_solution(5854917878601854711)
XLA Ops:
  0.0 30.1 %step.1 = (bf16[4,480,128]{2,1,0:T(8,128)(2,1)S(1)}, f32[4,128,128]{2,1,0:T(8,128)S(1)}, bf16[4,96,128]{2,1,0:T(8,128)(2,1)S(1)}, f32[9,2,128]{2,1,0:T(2,128)S(1...) custom-call(bf16[1,4,576,128]{3,2,1,0:T(8,128)(2,1)} %fields.1, ...), custom_call_target="tpu_custom_call" | custom-call | tf_op jit(solution)/shard_map/step/pallas_call | solution.py:430
  30.1 1.3 %finishing.1 = bf16[1,4,576,128]{3,2,1,0:T(8,128)(2,1)} custom-call(bf16[4,480,128]{2,1,0:T(8,128)(2,1)S(1)} %get-tuple-element.12.done, f32[4,128,128]{2,1,0:T(8,128)S(1)} %get-tuple-element.13.mix, bf16[4,96,128]{2,1,0:T(8,128)(2,1)S(1)} %get-tuple-element.14.old, f32[9,2,128]{2,1,0:T(2,128)S(1)} %get-tuple-element.15.lon32, ...), custom_call_target="tpu_custom_call" | custom-call | tf_op jit(solution)/shard_map/finishing/pallas_call | solution.py:454
